TPU v7x, 128 devices: a whole 4x4x4 slice. The times are simulated.
128 devices in a mesh: dp: 2 (over core), tensor: 4 (over y), context: 16 (over z, x).
Axes of the slice: x: 4, y: 4, z: 4, core: 2. Of those that a mesh axis runs over, the one named last changes fastest.
Arguments:
- ssm_input: bfloat16 [2, 4096, 4096], P('dp', 'context', 'tensor'), may hold values from -6 to 6
- gate_input: bfloat16 [2, 4096, 4096], P('dp', 'context', 'tensor'), may hold values from -6 to 6
- state_keys: bfloat16 [2, 4096, 1024], P('dp', 'context', 'tensor'), may hold values from -0.3984375 to 0.3984375
- state_queries: bfloat16 [2, 4096, 1024], P('dp', 'context', 'tensor'), may hold values from -0.3984375 to 0.3984375
- step_raw: float32 [2, 64, 4096], P('dp', 'tensor', 'context'), may hold values from -1 to 1.5
- rate_log: float32 [64], P('tensor'), may hold values from -13 to -2, as said below
- skip_gain: float32 [64], P('tensor'), may hold values from 0.5 to 2
- norm_gain: float32 [4096], P('tensor'), may hold values from 0.1 to 1.9
- out_weight: bfloat16 [4096, 4096], P(None, 'tensor'), may hold values from -0.09375 to 0.09375
- out_grad: bfloat16 [2, 4096, 4096], P('dp', 'context', 'tensor'), may hold values from -6 to 6
Outputs:
- grad_input: bfloat16 [2, 4096, 4096], P('dp', 'context', 'tensor')
- grad_gate: bfloat16 [2, 4096, 4096], P('dp', 'context', 'tensor')
- grad_keys: float32 [2, 4096, 1024], P('dp', 'context', 'tensor')
- grad_queries: float32 [2, 4096, 1024], P('dp', 'context', 'tensor')
- grad_step: float32 [2, 64, 4096], P('dp', 'tensor', 'context')
- grad_rate: float32 [64], P('tensor')
- grad_skip: float32 [64], P('tensor')
- grad_norm: float32 [4096], P('tensor')
- grad_weight: float32 [4096, 4096], P(('dp', 'context'), 'tensor')
Inputs may be any that keep to these rules, and one draw needn't show every extreme that they name: exp(rate_log) lies between 0.2 / 4096 and 1 / 12.
All inputs are finite; a program needn't handle non-finite values.
Results may differ from a plain program's by a relative error of at most 0.0029.
Values may be sent and summed in bfloat16 or wider, within the bound.
A program may use at most 128 MiB of HBM per device.

v0:
```python
import jax
import jax.numpy as jnp
from jax import lax
from jax.experimental import pallas as pl
from jax.experimental.pallas import tpu as pltpu
from jax.sharding import PartitionSpec as P

F32 = jnp.float32
BF = jnp.bfloat16
EPSILON = 1e-05
MESH = pl.DeviceIdType.MESH

T = 256
C = 1024
NH = 16
NQ = 8
W = 128
CTX = 16


def dot(a, b):
    return lax.dot_general(a, b, (((1,), (0,)), ((), ())), preferred_element_type=F32)


def dot_t(a, b):
    return lax.dot_general(a, b, (((1,), (1,)), ((), ())), preferred_element_type=F32)


def tdot(a, b):
    return lax.dot_general(a, b, (((0,), (0,)), ((), ())), preferred_element_type=F32)


def split2(v):
    hi = v.astype(BF)
    return hi, (v - hi.astype(F32)).astype(BF)


def split3(v):
    hi = v.astype(BF)
    rest = v - hi.astype(F32)
    mid = rest.astype(BF)
    return hi, mid, (rest - mid.astype(F32)).astype(BF)


def dot3(v, ones):
    parts = dot(jnp.concatenate(split3(v), axis=0), ones)
    return parts[0:NH] + parts[NH : 2 * NH] + parts[2 * NH : 3 * NH]


def iota(shape, axis):
    return lax.broadcasted_iota(jnp.int32, shape, axis)


def lanes(q):
    return pl.ds(pl.multiple_of(q * W, W), W)


def per_head(row):
    own = (iota((NH, C), 1) // 64) == iota((NH, C), 0)
    return jnp.sum(jnp.where(own, row, 0.0), axis=1, keepdims=True)


def kernel(
    x_ref, k_ref, q_ref, step_ref, rate_ref, skip_ref, gain_ref, gate_hbm, w_hbm, og_hbm,
    gi_hbm, gg_hbm, gk_hbm, gq_hbm, gs_hbm, sm_hbm, gw_hbm,
    gate_v, w_v, ogf, ogp, ogt, nm2,
    cumx, eexp, wexp, cum_s, stp_s, kt, qt, k2, q2, sc,
    snd, rcv, ent_s, ent, bsnd, brcv, out_s, outb,
    mt, phi, plo, y_s, gn_s, ga_s, g_s, acc, acc2, invb, mub,
    ds_s, dxw, dq_s, dk_s, rows, accr, accc, accv,
    gi_v, gg_v, gs_v, sm_own, sm_rcv, sm_sum, sm_p,
    sa, sb, owna, ownb, ra, rb, s2a, s2b, r2a, r2b, gw_v,
    in_sem, out_sem, og_ss, og_rs, fa_ss, fa_rs, fb_ss, fb_rs, ba_ss, ba_rs, bb_ss, bb_rs,
    p_ss, p_rs, r1_ss, r1_rs, r2_ss, r2_rs, m_ss, m_rs,
):
    me = lax.axis_index("context")
    myt = lax.axis_index("tensor")
    mydp = lax.axis_index("dp")
    mz, mx = me // 4, me % 4
    other = 1 - mydp
    right, left = (myt + 1) % 4, (myt + 3) % 4

    barrier = pltpu.get_barrier_semaphore()

    def greet(off, carry):
        pl.semaphore_signal(
            barrier, inc=1, device_id={"context": (me + off) % CTX}, device_id_type=MESH
        )
        return carry

    lax.fori_loop(1, CTX, greet, 0)
    pl.semaphore_signal(barrier, inc=1, device_id={"tensor": right}, device_id_type=MESH)
    pl.semaphore_signal(barrier, inc=1, device_id={"tensor": left}, device_id_type=MESH)
    pl.semaphore_signal(barrier, inc=1, device_id={"dp": other}, device_id_type=MESH)

    in_og = pltpu.make_async_copy(og_hbm, ogf.at[myt], in_sem.at[0])
    in_gate = pltpu.make_async_copy(gate_hbm, gate_v, in_sem.at[1])
    in_w = pltpu.make_async_copy(w_hbm, w_v, in_sem.at[2])
    in_og.start()
    in_gate.start()
    in_w.start()

    raw = step_ref[...]
    eye = iota((NH, NH), 0) == iota((NH, NH), 1)
    slope = jnp.sum(jnp.where(eye, jnp.exp(rate_ref[...]), 0.0), axis=1, keepdims=True)
    step = jnp.maximum(raw, 0.0) + jnp.log(1.0 + jnp.exp(-jnp.abs(raw)))
    decay = -slope * step
    upper = (iota((T, T), 0) <= iota((T, T), 1)).astype(BF)
    cum = dot3(decay, upper)
    total = cum[:, T - 1 : T]
    stp_s[...] = step
    cum_s[...] = cum
    spread = ((iota((3 * NH, C), 0) % NH) == (iota((3 * NH, C), 1) // 64)).astype(BF)

    def expand(v, to):
        pieces = jnp.concatenate(split3(v), axis=0).astype(F32)
        turned = jnp.concatenate([pieces, jnp.zeros((W - 3 * NH, T), F32)], axis=0).T
        to[...] = dot(turned[:, : 3 * NH].astype(BF), spread)

    expand(jnp.exp(cum), eexp)
    expand(jnp.exp(total - cum) * step, wexp)
    expand(cum, cumx)
    own = (iota((NH, C), 1) // 64) == iota((NH, C), 0)
    skip_col = jnp.sum(jnp.where(eye, skip_ref[...], 0.0), axis=1, keepdims=True)
    rows[3] = jnp.sum(jnp.where(own, skip_col, 0.0), axis=0, keepdims=True)

    for g in range(2):
        kg = k_ref[:, g * W : (g + 1) * W]
        qg = q_ref[:, g * W : (g + 1) * W]
        kt[g] = kg.T
        qt[g] = qg.T
        k2[g] = jnp.concatenate([kg, kg], axis=1)
        q2[g] = jnp.concatenate([qg, qg], axis=1)

    def local_state(q, carry):
        hi, lo = split2(x_ref[:, lanes(q)].astype(F32) * wexp[:, lanes(q)])
        both = dot(kt[q // 4], jnp.concatenate([hi, lo], axis=1))
        state = both[:, :W] + both[:, W:]
        factor = jnp.broadcast_to(eexp[T - 1 : T, lanes(q)], (8, W))
        snd[2 * q, 0:64] = state[0:64]
        snd[2 * q + 1, 0:64] = state[64:]
        snd[2 * q, 64:72] = factor
        snd[2 * q + 1, 64:72] = factor
        return carry

    lax.fori_loop(0, NQ, local_state, 0)

    pl.semaphore_wait(barrier, CTX + 2)

    def ctx_copy(src, dst, ss, rs, peer, src_slot, dst_slot):
        return pltpu.make_async_remote_copy(
            src_ref=src.at[src_slot],
            dst_ref=dst.at[dst_slot],
            send_sem=ss.at[src_slot],
            recv_sem=rs.at[dst_slot],
            device_id={"context": peer},
            device_id_type=MESH,
        )

    def send_all(src, dst, ss, rs):
        def one(off, carry):
            peer = (me + off) % CTX
            ctx_copy(src, dst, ss, rs, peer, peer, me).start()
            return carry

        lax.fori_loop(1, CTX, one, 0)

    def recv_all(src, dst, ss, rs):
        def one(off, carry):
            peer = (me + off) % CTX
            ctx_copy(src, dst, ss, rs, peer, peer, peer).wait_recv()
            return carry

        lax.fori_loop(1, CTX, one, 0)

    def drain_all(src, dst, ss, rs):
        def one(off, carry):
            peer = (me + off) % CTX
            ctx_copy(src, dst, ss, rs, peer, peer, me).wait_send()
            return carry

        lax.fori_loop(1, CTX, one, 0)

    send_all(snd, rcv, fa_ss, fa_rs)

    def ring(src, dst, sem, peer):
        return pltpu.make_async_remote_copy(
            src_ref=src,
            dst_ref=dst,
            send_sem=og_ss.at[sem],
            recv_sem=og_rs.at[sem],
            device_id={"tensor": peer},
            device_id_type=MESH,
        )

    to_right = ring(og_hbm, ogf.at[myt], 0, right)
    to_left = ring(og_hbm, ogf.at[myt], 1, left)
    to_right.start()
    to_left.start()

    for g in range(2):
        sc[g] = dot_t(q_ref[:, g * W : (g + 1) * W], k_ref[:, g * W : (g + 1) * W])
    causal = iota((T, T), 0) >= iota((T, T), 1)
    first = iota((T, W), 1) < 64

    def within(q, carry):
        xp = x_ref[:, lanes(q)]
        spread_tile = cumx[:, lanes(q)]
        outs = []
        for hh in range(2):
            h = 2 * q + hh
            column = spread_tile[:, 64 * hh : 64 * hh + 1]
            gap = column - cum_s[pl.ds(h, 1), :]
            m = jnp.exp(jnp.where(causal, gap, -1e30)) * stp_s[pl.ds(h, 1), :]
            mt[h] = m
            hi, lo = split2(m * sc[q // 4])
            phi[h] = hi
            plo[h] = lo
            outs.append(dot(hi, xp) + dot(lo, xp))
        y_s[:, lanes(q)] = jnp.where(first, outs[0], outs[1])
        return carry

    lax.fori_loop(0, NQ, within, 0)

    rcv[me] = snd[me]
    recv_all(snd, rcv, fa_ss, fa_rs)
    run = jnp.zeros((64, W), F32)
    for s in range(CTX):
        ent_s[s] = run
        run = rcv[s, 64:65, :] * run + rcv[s, 0:64, :]
    send_all(ent_s, ent, fb_ss, fb_rs)
    ent[me] = ent_s[me]

    in_og.wait()
    to_right.wait_recv()
    relay_right = ring(ogf.at[left, 0:128], ogf.at[left, 0:128], 2, right)
    relay_right.start()
    to_left.wait_recv()
    relay_left = ring(ogf.at[right, 128:256], ogf.at[right, 128:256], 3, left)
    relay_left.start()
    in_w.wait()

    def project(chunk, first_term):
        def one(n, carry):
            part = dot(
                ogf[chunk], w_v[pl.ds(pl.multiple_of(chunk * C, C), C), pl.ds(pl.multiple_of(n * 256, 256), 256)]
            )
            where = pl.ds(pl.multiple_of(n * 256, 256), 256)
            gn_s[:, where] = part if first_term else gn_s[:, where] + part
            return carry

        lax.fori_loop(0, 4, one, 0)

    project(myt, True)
    project(left, False)
    project(right, False)
    relay_right.wait_recv()
    relay_left.wait_recv()

    def pair(src, dst, sem):
        return pltpu.make_async_remote_copy(
            src_ref=src,
            dst_ref=dst,
            send_sem=p_ss.at[sem],
            recv_sem=p_rs.at[sem],
            device_id={"dp": other},
            device_id_type=MESH,
        )

    pair_og = [pair(ogf.at[2 * other + i], ogp.at[i], i) for i in range(2)]
    for copy in pair_og:
        copy.start()
    project((myt + 2) % 4, False)

    def turn_own(i, carry):
        at = pl.ds(pl.multiple_of(i * W, W), W)
        ogt[at, 0:T] = ogf[2 * mydp + i // 8, :, lanes(i % 8)].T
        return carry

    lax.fori_loop(0, 16, turn_own, 0)
    for copy in pair_og:
        copy.wait_recv()

    def turn_pair(i, carry):
        at = pl.ds(pl.multiple_of(i * W, W), W)
        ogt[at, T : 2 * T] = ogp[i // 8, :, lanes(i % 8)].T
        return carry

    lax.fori_loop(0, 16, turn_pair, 0)
    in_gate.wait()
    recv_all(ent_s, ent, fb_ss, fb_rs)

    acc[...] = jnp.zeros_like(acc)
    acc2[...] = jnp.zeros_like(acc2)

    def entering(q):
        return jnp.concatenate([ent[2 * q], ent[2 * q + 1]], axis=0)

    def scan_out(q, carry):
        g = q // 4
        carried = dot(q2[g], jnp.concatenate(split2(entering(q)), axis=0))
        y = y_s[:, lanes(q)] + eexp[:, lanes(q)] * carried
        y_s[:, lanes(q)] = y
        ssd = y + rows[3, :, lanes(q)] * x_ref[:, lanes(q)].astype(F32)
        gate = gate_v[:, lanes(q)].astype(F32)
        gated = ssd * (gate / (1.0 + jnp.exp(-gate)))
        ga_s[:, lanes(q)] = gated
        acc[g] += gated * gated
        acc2[g] += gn_s[:, lanes(q)] * gain_ref[:, lanes(q)] * gated
        return carry

    lax.fori_loop(0, NQ, scan_out, 0)
    for g in range(2):
        mean = jnp.sum(acc[g], axis=1, keepdims=True) * (1.0 / 512)
        inverse = lax.rsqrt(mean + EPSILON)
        shift = jnp.sum(acc2[g], axis=1, keepdims=True) * (1.0 / 512)
        invb[g] = jnp.broadcast_to(inverse, (T, W))
        mub[g] = jnp.broadcast_to(shift * inverse * inverse, (T, W))

    def normalize(q, carry):
        value = ga_s[:, lanes(q)] * invb[q // 4] * gain_ref[:, lanes(q)]
        nm2[0:T, lanes(q)] = value.astype(BF)
        return carry

    lax.fori_loop(0, NQ, normalize, 0)
    pair_nm = pair(nm2.at[0:T], nm2.at[T : 2 * T], 2)
    pair_nm.start()

    def norm_back(q, carry):
        g = q // 4
        gated = ga_s[:, lanes(q)]
        inverse = invb[g]
        gn = gn_s[:, lanes(q)]
        d_gated = inverse * (gn * gain_ref[:, lanes(q)] - gated * mub[g])
        rows[0, :, lanes(q)] = jnp.sum(gn * gated * inverse, axis=0, keepdims=True)
        gate = gate_v[:, lanes(q)].astype(F32)
        xv = x_ref[:, lanes(q)].astype(F32)
        sig = 1.0 / (1.0 + jnp.exp(-gate))
        silu = gate * sig
        y = y_s[:, lanes(q)]
        ssd = y + rows[3, :, lanes(q)] * xv
        gg_v[:, lanes(q)] = (d_gated * ssd * (sig * (1.0 + gate - silu))).astype(BF)
        grad = d_gated * silu
        g_s[:, lanes(q)] = grad
        rows[1, :, lanes(q)] = jnp.sum(grad * xv, axis=0, keepdims=True)
        hi, lo = split2(eexp[:, lanes(q)] * grad)
        both = dot(qt[g], jnp.concatenate([hi, lo], axis=1))
        into = both[:, :W] + both[:, W:]
        bsnd[2 * q] = into[0:64]
        bsnd[2 * q + 1] = into[64:]
        return carry

    lax.fori_loop(0, NQ, norm_back, 0)
    out_gg = pltpu.make_async_copy(gg_v, gg_hbm, out_sem.at[0])
    out_gg.start()
    send_all(bsnd, brcv, ba_ss, ba_rs)

    pair_nm.wait_recv()

    def weight_block(block, half):
        at = pl.ds(pl.multiple_of(block * W, W), W)
        return dot(ogt[at, :], nm2[:, half * 512 : half * 512 + 512])

    def phase1(src, dst, sem, peer):
        return pltpu.make_async_remote_copy(
            src_ref=src,
            dst_ref=dst,
            send_sem=r1_ss.at[sem],
            recv_sem=r1_rs.at[sem],
            device_id={"context": peer},
            device_id_type=MESH,
        )

    def phase2(src, dst, sem, peer):
        return pltpu.make_async_remote_copy(
            src_ref=src,
            dst_ref=dst,
            send_sem=r2_ss.at[sem],
            recv_sem=r2_rs.at[sem],
            device_id={"context": peer},
            device_id_type=MESH,
        )

    sends1 = []
    for d in (2, 1, 3):
        px = (mx + d) % 4
        pz = (mz + d) % 4

        def fill_a(i, carry, px=px, d=d):
            sa[d - 1, i] = weight_block(i * 4 + px, 0).astype(BF)
            return carry

        lax.fori_loop(0, 4, fill_a, 0)
        copy = phase1(sa.at[d - 1], ra.at[d - 1], d - 1, mz * 4 + px)
        copy.start()
        sends1.append(copy)

        def fill_b(i, carry, pz=pz, d=d):
            sb[d - 1, i] = weight_block(pz * 4 + i, 1).astype(BF)
            return carry

        lax.fori_loop(0, 4, fill_b, 0)
        copy = phase1(sb.at[d - 1], rb.at[d - 1], 3 + d - 1, pz * 4 + mx)
        copy.start()
        sends1.append(copy)

    def fill_own(i, carry):
        owna[i] = weight_block(i * 4 + mx, 0)
        ownb[i] = weight_block(mz * 4 + i, 1)
        return carry

    lax.fori_loop(0, 4, fill_own, 0)

    brcv[me] = bsnd[me]
    recv_all(bsnd, brcv, ba_ss, ba_rs)
    run = jnp.zeros((64, W), F32)
    for s in range(CTX - 1, -1, -1):
        out_s[s] = run
        run = brcv[s] + rcv[s, 64:65, :] * run
    send_all(out_s, outb, bb_ss, bb_rs)
    outb[me] = out_s[me]

    ds_s[...] = jnp.zeros_like(ds_s)
    dq_s[...] = jnp.zeros_like(dq_s)
    dk_s[...] = jnp.zeros_like(dk_s)
    accr[...] = jnp.zeros_like(accr)
    accc[...] = jnp.zeros_like(accc)
    accv[...] = jnp.zeros_like(accv)

    def head_sums(q, value):
        row, lane = iota((NH, 2 * W), 0), iota((NH, 2 * W), 1) % W
        pick = (row == 2 * q + lane // 64).astype(BF)
        return dot_t(pick, jnp.concatenate(split2(value), axis=1))

    def within_back(q, carry):
        g = q // 4
        xp = x_ref[:, lanes(q)]
        grad = g_s[:, lanes(q)]
        ghi, glo = split2(grad)
        gthi, gtlo = ghi.T, glo.T
        x2 = jnp.concatenate([xp, xp], axis=1)
        zero = jnp.zeros((T, W), BF)
        parts = []
        total_ds = ds_s[g]
        for hh in range(2):
            h = 2 * q + hh
            keep = first if hh == 0 else jnp.logical_not(first)
            g2 = jnp.concatenate([jnp.where(keep, ghi, zero), jnp.where(keep, glo, zero)], axis=1)
            total_ds = total_ds + dot_t(g2, x2) * mt[h]
            a, b = gthi[64 * hh : 64 * hh + 64], gtlo[64 * hh : 64 * hh + 64]
            both = dot(jnp.concatenate([a, b], axis=0), phi[h])
            parts.append(both[0:64] + both[64:] + dot(a, plo[h]))
        ds_s[g] = total_ds
        dxw[:, lanes(q)] = jnp.concatenate(parts, axis=0).T
        accr[...] += head_sums(q, grad * y_s[:, lanes(q)])
        ehi, elo = split2(eexp[:, lanes(q)] * grad)
        shi, slo = split2(entering(q))
        to_q = dot_t(jnp.concatenate([ehi, elo], axis=1), jnp.concatenate([shi, shi], axis=1))
        dq_s[:, lanes(g)] += to_q + dot_t(ehi, slo)
        return carry

    lax.fori_loop(0, NQ, within_back, 0)
    for g in range(2):
        hi, lo = split2(ds_s[g])
        kg = k_ref[:, g * W : (g + 1) * W]
        qg = q_ref[:, g * W : (g + 1) * W]
        dq_s[:, g * W : (g + 1) * W] += dot(hi, kg) + dot(lo, kg)
        dk_s[:, g * W : (g + 1) * W] = tdot(hi, qg) + tdot(lo, qg)
    out_gq = pltpu.make_async_copy(dq_s, gq_hbm, out_sem.at[1])
    out_gq.start()

    recv_all(out_s, outb, bb_ss, bb_rs)

    def state_back(q, carry):
        g = q // 4
        d_state = jnp.concatenate([outb[2 * q], outb[2 * q + 1]], axis=0)
        dhi, dlo = split2(d_state)
        rows[2, :, lanes(q)] = jnp.sum(d_state * entering(q), axis=0, keepdims=True)
        weight = wexp[:, lanes(q)]
        xv = x_ref[:, lanes(q)].astype(F32)
        via = weight * dot(k2[g], jnp.concatenate([dhi, dlo], axis=0))
        dx = dxw[:, lanes(q)] + via
        gi_v[:, lanes(q)] = (dx + rows[3, :, lanes(q)] * g_s[:, lanes(q)]).astype(BF)
        accc[...] += head_sums(q, xv * dx)
        accv[...] += head_sums(q, xv * via)
        whi, wlo = split2(weight * xv)
        to_k = dot_t(jnp.concatenate([whi, wlo], axis=1), jnp.concatenate([dhi, dhi], axis=1))
        dk_s[:, lanes(g)] += to_k + dot_t(whi, dlo)
        return carry

    lax.fori_loop(0, NQ, state_back, 0)
    out_gi = pltpu.make_async_copy(gi_v, gi_hbm, out_sem.at[2])
    out_gi.start()
    out_gk = pltpu.make_async_copy(dk_s, gk_hbm, out_sem.at[3])
    out_gk.start()

    raw = step_ref[...]
    slope = jnp.sum(jnp.where(eye, jnp.exp(rate_ref[...]), 0.0), axis=1, keepdims=True)
    step = stp_s[...]
    lower = (iota((T, T), 0) >= iota((T, T), 1)).astype(BF)
    after = dot3(accr[...] - accc[...], lower)
    log_grad = per_head(rows[2] * eexp[T - 1 : T, :])
    d_total = jnp.sum(accv[...], axis=1, keepdims=True) + log_grad
    d_decay = after + d_total
    gs_v[...] = (accc[...] / step - slope * d_decay) / (1.0 + jnp.exp(-raw))
    out_gs = pltpu.make_async_copy(gs_v, gs_hbm, out_sem.at[4])
    out_gs.start()
    rate_part = jnp.sum(d_decay * (-slope * step), axis=1, keepdims=True)
    lane = iota((NH, W), 1)
    sm_own[0:NH] = jnp.where(lane == 0, rate_part, jnp.where(lane == 1, per_head(rows[1]), 0.0))
    for i in range(NQ):
        sm_own[NH + i : NH + i + 1] = rows[0, :, i * W : (i + 1) * W]

    def small_copy(peer, slot):
        return pltpu.make_async_remote_copy(
            src_ref=sm_own,
            dst_ref=sm_rcv.at[slot],
            send_sem=m_ss.at[peer],
            recv_sem=m_rs.at[slot],
            device_id={"context": peer},
            device_id_type=MESH,
        )

    def small_send(off, carry):
        small_copy((me + off) % CTX, me).start()
        return carry

    def small_recv(off, carry):
        small_copy((me + off) % CTX, (me + off) % CTX).wait_recv()
        return carry

    def small_drain(off, carry):
        small_copy((me + off) % CTX, me).wait_send()
        return carry

    lax.fori_loop(1, CTX, small_send, 0)
    sm_rcv[me] = sm_own[...]

    for d in (1, 3, 2):
        phase1(sa.at[d - 1], ra.at[d - 1], d - 1, mz * 4 + mx).wait_recv()
        phase1(sb.at[d - 1], rb.at[d - 1], 3 + d - 1, mz * 4 + mx).wait_recv()

    def sum_a(i):
        value = owna[i]
        for d in range(3):
            value = value + ra[d, i].astype(F32)
        return value

    def sum_b(i):
        value = ownb[i]
        for d in range(3):
            value = value + rb[d, i].astype(F32)
        return value

    sends2 = []
    for d in (2, 1, 3):
        pz = (mz + d) % 4
        px = (mx + d) % 4
        s2a[d - 1] = sum_a(pz).astype(BF)
        copy = phase2(s2a.at[d - 1], r2a.at[d - 1], d - 1, pz * 4 + mx)
        copy.start()
        sends2.append(copy)
        s2b[d - 1] = sum_b(px).astype(BF)
        copy = phase2(s2b.at[d - 1], r2b.at[d - 1], 3 + d - 1, mz * 4 + px)
        copy.start()
        sends2.append(copy)
    gw_v[:, 0:512] = sum_a(mz)
    gw_v[:, 512:1024] = sum_b(mx)

    lax.fori_loop(1, CTX, small_recv, 0)
    value = sm_rcv[0]
    for s in range(1, CTX):
        value = value + sm_rcv[s]
    sm_sum[...] = value
    pair_sm = pair(sm_sum, sm_p, 3)
    pair_sm.start()

    for copy in sends2:
        copy.wait_recv()
    for d in range(3):
        gw_v[:, 0:512] += r2a[d].astype(F32)
        gw_v[:, 512:1024] += r2b[d].astype(F32)
    out_gw = pltpu.make_async_copy(gw_v, gw_hbm, out_sem.at[5])
    out_gw.start()

    pair_sm.wait()
    sm_sum[...] += sm_p[...]
    out_sm = pltpu.make_async_copy(sm_sum, sm_hbm, out_sem.at[6])
    out_sm.start()

    drain_all(snd, rcv, fa_ss, fa_rs)
    drain_all(ent_s, ent, fb_ss, fb_rs)
    drain_all(bsnd, brcv, ba_ss, ba_rs)
    drain_all(out_s, outb, bb_ss, bb_rs)
    lax.fori_loop(1, CTX, small_drain, 0)
    for copy in (to_right, to_left, relay_right, relay_left, *pair_og, pair_nm, *sends1, *sends2):
        copy.wait_send()
    for copy in (out_gg, out_gq, out_gi, out_gk, out_gs, out_gw, out_sm):
        copy.wait()


def body(
    ssm_input, gate_input, state_keys, state_queries, step_raw,
    rate_log, skip_gain, norm_gain, out_weight, out_grad,
):
    vmem, anywhere = pl.BlockSpec(memory_space=pltpu.VMEM), pl.BlockSpec(memory_space=pl.ANY)
    V, S = pltpu.VMEM, pltpu.SemaphoreType.DMA
    scratch = [
        V((T, C), BF), V((4 * C, C), BF), V((4, T, C), BF), V((2, T, C), BF), V((2 * C, 2 * T), BF),
        V((2 * T, C), BF),
        V((T, C), F32), V((T, C), F32), V((T, C), F32), V((NH, T), F32), V((NH, T), F32),
        V((2, W, T), BF), V((2, W, T), BF), V((2, T, 2 * W), BF), V((2, T, 2 * W), BF),
        V((2, T, T), F32),
        V((CTX, 72, W), F32), V((CTX, 72, W), F32), V((CTX, 64, W), F32), V((CTX, 64, W), F32),
        V((CTX, 64, W), F32), V((CTX, 64, W), F32), V((CTX, 64, W), F32), V((CTX, 64, W), F32),
        V((NH, T, T), F32), V((NH, T, T), BF), V((NH, T, T), BF),
        V((T, C), F32), V((T, C), F32), V((T, C), F32), V((T, C), F32),
        V((2, T, W), F32), V((2, T, W), F32), V((2, T, W), F32), V((2, T, W), F32),
        V((2, T, T), F32), V((T, C), F32), V((T, 2 * W), F32), V((T, 2 * W), F32),
        V((4, 1, C), F32), V((NH, T), F32), V((NH, T), F32), V((NH, T), F32),
        V((T, C), BF), V((T, C), BF), V((NH, T), F32),
        V((24, W), F32), V((CTX, 24, W), F32), V((24, W), F32), V((24, W), F32),
        V((3, 4, W, 512), BF), V((3, 4, W, 512), BF), V((4, W, 512), F32), V((4, W, 512), F32),
        V((3, 4, W, 512), BF), V((3, 4, W, 512), BF),
        V((3, W, 512), BF), V((3, W, 512), BF), V((3, W, 512), BF), V((3, W, 512), BF),
        V((W, C), F32),
        S((3,)), S((7,)), S((4,)), S((4,)),
        S((CTX,)), S((CTX,)), S((CTX,)), S((CTX,)), S((CTX,)), S((CTX,)), S((CTX,)), S((CTX,)),
        S((4,)), S((4,)), S((6,)), S((6,)), S((6,)), S((6,)), S((CTX,)), S((CTX,)),
    ]
    gi, gg, gk, gq, gs, sm, gw = pl.pallas_call(
        kernel,
        out_shape=(
            jax.ShapeDtypeStruct((T, C), BF),
            jax.ShapeDtypeStruct((T, C), BF),
            jax.ShapeDtypeStruct((T, 2 * W), F32),
            jax.ShapeDtypeStruct((T, 2 * W), F32),
            jax.ShapeDtypeStruct((NH, T), F32),
            jax.ShapeDtypeStruct((24, W), F32),
            jax.ShapeDtypeStruct((W, C), F32),
        ),
        in_specs=[vmem] * 7 + [anywhere] * 3,
        out_specs=[anywhere] * 7,
        scratch_shapes=scratch,
        compiler_params=pltpu.CompilerParams(
            collective_id=0, has_side_effects=True, vmem_limit_bytes=60 * 1024 * 1024
        ),
    )(
        ssm_input[0], state_keys[0], state_queries[0], step_raw[0],
        rate_log.reshape(1, NH), skip_gain.reshape(1, NH), norm_gain.reshape(1, C),
        gate_input[0], out_weight, out_grad[0],
    )
    return (
        gi[None], gg[None], gk[None], gq[None], gs[None],
        sm[0:NH, 0], sm[0:NH, 1], sm[NH:24].reshape(C), gw,
    )


def solution(mesh):
    return jax.shard_map(
        body,
        mesh=mesh,
        in_specs=(
            P("dp", "context", "tensor"),
            P("dp", "context", "tensor"),
            P("dp", "context", "tensor"),
            P("dp", "context", "tensor"),
            P("dp", "tensor", "context"),
            P("tensor"),
            P("tensor"),
            P("tensor"),
            P(None, "tensor"),
            P("dp", "context", "tensor"),
        ),
        out_specs=(
            P("dp", "context", "tensor"),
            P("dp", "context", "tensor"),
            P("dp", "context", "tensor"),
            P("dp", "context", "tensor"),
            P("dp", "tensor", "context"),
            P("tensor"),
            P("tensor"),
            P("tensor"),
            P(("dp", "context"), "tensor"),
        ),
        check_vma=False,
    )
```

profile of v0, /device:TPU:1, one launch (start us, length us, event | category | flops | bytes accessed | tf_op | source)
XLA Modules:
  0.0 105.1 jit_solution(3029797819615170711)
XLA Ops:
  0.6 91.5 %shard_map.169 = (bf16[256,1024]{1,0:T(8,128)(2,1)}, bf16[256,1024]{1,0:T(8,128)(2,1)}, f32[256,256]{1,0:T(8,128)}, f32[256,256]{1,0:T(8,128)}, f32[16,256]{1,0:...) custom-call(bf16[256,1024]{1,0:T(8,128)(2,1)} %bitcast.16, bf16[256,256]{1,0:T(8,128)(2,1)} %bitcast.23, ...), custom_call_target="tpu_custom_call" | custom-call | tf_op jit(solution)/shard_map/pallas_call | solution.py:631
  92.1 1.5 %slice_reduce_fusion = (f32[16]{0:T(128)}, f32[16]{0:T(128)}) fusion(f32[24,128]{1,0:T(8,128)} %get-tuple-element.21), kind=kLoop, calls=%fused_computation | loop fusion | bytes 256 | tf_op jit(solution)/shard_map/slice | solution.py:655
  93.6 1.3 %slice_bitcast_fusion = f32[1024]{0:T(1024)} fusion(f32[24,128]{1,0:T(8,128)} %get-tuple-element.21), kind=kLoop, calls=%fused_computation.2 | loop fusion | bytes 8192 | tf_op jit(solution)/shard_map/reshape | solution.py:655
  94.9 1.9 %copy.25 = bf16[1,256,1024]{2,1,0:T(8,128)(2,1)} copy(bf16[1,256,1024]{2,1,0:T(8,128)(2,1)} %bitcast.20) | data formatting | bytes 1048576
  96.7 1.9 %copy.26 = bf16[1,256,1024]{2,1,0:T(8,128)(2,1)} copy(bf16[1,256,1024]{2,1,0:T(8,128)(2,1)} %bitcast.19) | data formatting | bytes 1048576
  98.6 1.7 %copy.27 = f32[1,256,256]{2,1,0:T(8,128)} copy(f32[1,256,256]{2,1,0:T(8,128)} %bitcast.22) | data formatting | bytes 524288
  100.3 1.7 %copy.28 = f32[1,256,256]{2,1,0:T(8,128)} copy(f32[1,256,256]{2,1,0:T(8,128)} %bitcast.21) | data formatting | bytes 524288
  101.9 1.3 %copy.29 = f32[1,16,256]{2,1,0:T(8,128)} copy(f32[1,16,256]{2,1,0:T(8,128)} %bitcast.26) | data formatting | bytes 32768
  103.3 1.9 %copy.30 = f32[128,1024]{1,0:T(8,128)} copy(f32[128,1024]{1,0:T(8,128)} %get-tuple-element.42) | data formatting | bytes 1048576
where the time goes:
time: 106 us; the launch traced here: 105 us
  Pallas kernels  91.5 us (86%)
  local copies, waits for them, and re-layouts  13 us (12%)
    pallas_call x1, Pallas kernels, body(): pl.pallas_call(kernel, out_shape=(jax.ShapeDtypeStruct((T, C), BF), jax.S...  91.5 us
    unnamed x6, local copies, waits for them, and re-layouts  10.3 us

commit v1 on v0

--- a/solution.py
+++ b/solution.py
@@ -596,6 +596,35 @@
     for copy in (to_right, to_left, relay_right, relay_left, *pair_og, pair_nm, *sends1, *sends2):
         copy.wait_send()
     for copy in (out_gg, out_gq, out_gi, out_gk, out_gs, out_gw, out_sm):
+        copy.wait()
+
+
+def hand_out(
+    gi_in, gg_in, gk_in, gq_in, gs_in, sm_in, gw_in,
+    gi_out, gg_out, gk_out, gq_out, gs_out, gw_out, rate_ref, skip_ref, norm_ref,
+    gi_v, gg_v, gk_v, gq_v, gs_v, gw_v, sm_v, in_sem, out_sem,
+):
+    small = pltpu.make_async_copy(sm_in, sm_v, in_sem.at[6])
+    small.start()
+    ways = (
+        (gi_in, gi_v, gi_out), (gg_in, gg_v, gg_out), (gw_in, gw_v, gw_out),
+        (gk_in, gk_v, gk_out), (gq_in, gq_v, gq_out), (gs_in, gs_v, gs_out),
+    )
+    into = [pltpu.make_async_copy(w[0], w[1], in_sem.at[i]) for i, w in enumerate(ways)]
+    out = [pltpu.make_async_copy(w[1], w[2], out_sem.at[i]) for i, w in enumerate(ways)]
+    for copy in into:
+        copy.start()
+    small.wait()
+    eye = iota((NH, W), 0) == iota((NH, W), 1)
+    for lane, ref in ((0, rate_ref), (1, skip_ref)):
+        column = sm_v[0:NH, lane : lane + 1]
+        ref[...] = jnp.sum(jnp.where(eye, column, 0.0), axis=0, keepdims=True)[:, 0:NH]
+    for i in range(NQ):
+        norm_ref[:, i * W : (i + 1) * W] = sm_v[NH + i : NH + i + 1]
+    for before, after in zip(into, out):
+        before.wait()
+        after.start()
+    for copy in out:
         copy.wait()
 
 
@@ -628,7 +657,7 @@
         S((CTX,)), S((CTX,)), S((CTX,)), S((CTX,)), S((CTX,)), S((CTX,)), S((CTX,)), S((CTX,)),
         S((4,)), S((4,)), S((6,)), S((6,)), S((6,)), S((6,)), S((CTX,)), S((CTX,)),
     ]
-    gi, gg, gk, gq, gs, sm, gw = pl.pallas_call(
+    parts = pl.pallas_call(
         kernel,
         out_shape=(
             jax.ShapeDtypeStruct((T, C), BF),
@@ -650,9 +679,29 @@
         rate_log.reshape(1, NH), skip_gain.reshape(1, NH), norm_gain.reshape(1, C),
         gate_input[0], out_weight, out_grad[0],
     )
+    gi, gg, gk, gq, gs, gw, rate, skip, norm = pl.pallas_call(
+        hand_out,
+        out_shape=(
+            jax.ShapeDtypeStruct((T, C), BF),
+            jax.ShapeDtypeStruct((T, C), BF),
+            jax.ShapeDtypeStruct((T, 2 * W), F32),
+            jax.ShapeDtypeStruct((T, 2 * W), F32),
+            jax.ShapeDtypeStruct((NH, T), F32),
+            jax.ShapeDtypeStruct((W, C), F32),
+            jax.ShapeDtypeStruct((1, NH), F32),
+            jax.ShapeDtypeStruct((1, NH), F32),
+            jax.ShapeDtypeStruct((1, C), F32),
+        ),
+        in_specs=[anywhere] * 7,
+        out_specs=[anywhere] * 6 + [vmem] * 3,
+        scratch_shapes=[
+            V((T, C), BF), V((T, C), BF), V((T, 2 * W), F32), V((T, 2 * W), F32), V((NH, T), F32),
+            V((W, C), F32), V((24, W), F32), S((7,)), S((6,)),
+        ],
+    )(*parts)
     return (
         gi[None], gg[None], gk[None], gq[None], gs[None],
-        sm[0:NH, 0], sm[0:NH, 1], sm[NH:24].reshape(C), gw,
+        rate.reshape(NH), skip.reshape(NH), norm.reshape(C), gw,
     )
 
 

time: 106 us -> 95.4 us (0.900)
  local copies, waits for them, and re-layouts: 13 us -> 0 us
  Pallas kernels: 91.5 us -> 94.6 us
    unnamed x6 -> x0, local copies, waits for them, and re-layouts: 10.3 us -> none
    pallas_call x0 -> x1, Pallas kernels: none -> 3.08 us  [body(): pl.pallas_call(hand_out, out_shape=(jax.ShapeDtypeStruct((T, C), BF), jax...]
    slice x1 -> x0, local copies, waits for them, and re-layouts: 1.47 us -> none  [body(): sm[0:NH, 1]]
    reshape x1 -> x0, local copies, waits for them, and re-layouts: 1.27 us -> none  [body(): sm[NH:24].reshape(C)]
where the time goes in v1:
time: 95.4 us; the launch traced here: 95.2 us
  Pallas kernels  94.6 us (99%)
    pallas_call x1, Pallas kernels, body(): pl.pallas_call(kernel, out_shape=(jax.ShapeDtypeStruct((T, C), BF), jax.S...  91.5 us
    pallas_call x1, Pallas kernels, body(): pl.pallas_call(hand_out, out_shape=(jax.ShapeDtypeStruct((T, C), BF), jax...  3.08 us

profile of v1, /device:TPU:1, one launch (start us, length us, event | category | flops | bytes accessed | tf_op | source)
XLA Modules:
  0.0 95.2 jit_solution(15103256837939778251)
XLA Ops:
  0.6 91.5 %shard_map.169 = (bf16[256,1024]{1,0:T(8,128)(2,1)}, bf16[256,1024]{1,0:T(8,128)(2,1)}, f32[256,256]{1,0:T(8,128)}, f32[256,256]{1,0:T(8,128)}, f32[16,256]{1,0:...) custom-call(bf16[256,1024]{1,0:T(8,128)(2,1)} %bitcast.17, bf16[256,256]{1,0:T(8,128)(2,1)} %bitcast.20, ...), custom_call_target="tpu_custom_call" | custom-call | tf_op jit(solution)/shard_map/pallas_call | solution.py:660
  92.1 3.1 %shard_map.170 = (bf16[256,1024]{1,0:T(8,128)(2,1)}, bf16[256,1024]{1,0:T(8,128)(2,1)}, f32[256,256]{1,0:T(8,128)}, f32[256,256]{1,0:T(8,128)}, f32[16,256]{1,0:...) custom-call(bf16[256,1024]{1,0:T(8,128)(2,1)} %get-tuple-element.25.gi_in, ...), custom_call_target="tpu_custom_call" | custom-call | tf_op jit(solution)/shard_map/pallas_call | solution.py:682

commit v2 on v0

v2 whole, which is shorter than its diff:
```python
import jax
import jax.numpy as jnp
from jax import lax
from jax.experimental import pallas as pl
from jax.experimental.pallas import tpu as pltpu
from jax.sharding import PartitionSpec as P

F32 = jnp.float32
BF = jnp.bfloat16
EPSILON = 1e-05
MESH = pl.DeviceIdType.MESH

T = 256
C = 1024
NH = 16
NQ = 8
W = 128
CTX = 16


def dot(a, b):
    return lax.dot_general(a, b, (((1,), (0,)), ((), ())), preferred_element_type=F32)


def dot_t(a, b):
    return lax.dot_general(a, b, (((1,), (1,)), ((), ())), preferred_element_type=F32)


def tdot(a, b):
    return lax.dot_general(a, b, (((0,), (0,)), ((), ())), preferred_element_type=F32)


def split2(v):
    hi = v.astype(BF)
    return hi, (v - hi.astype(F32)).astype(BF)


def split3(v):
    hi = v.astype(BF)
    rest = v - hi.astype(F32)
    mid = rest.astype(BF)
    return hi, mid, (rest - mid.astype(F32)).astype(BF)


def dot3(v, ones):
    parts = dot(jnp.concatenate(split3(v), axis=0), ones)
    return parts[0:NH] + parts[NH : 2 * NH] + parts[2 * NH : 3 * NH]


def iota(shape, axis):
    return lax.broadcasted_iota(jnp.int32, shape, axis)


def lanes(q):
    return pl.ds(pl.multiple_of(q * W, W), W)


def per_head(row):
    own = (iota((NH, C), 1) // 64) == iota((NH, C), 0)
    return jnp.sum(jnp.where(own, row, 0.0), axis=1, keepdims=True)


def kernel(
    x_hbm, k_hbm, q_hbm, step_hbm, rate_hbm, skip_hbm, gain_hbm, gate_hbm, w_hbm, og_hbm,
    gi_v, gg_v, dk_s, dq_s, gs_v, gw_v, ea_own, la_own,
    x_ref, k_ref, q_ref, step_ref, rate_ref, skip_ref, gain_ref,
    gate_v, w_v, ogf, ogp, ogt, nm2,
    cumx, eexp, wexp, cum_s, stp_s, kt, qt, sc,
    snd, rcv, ent_s, ent, bsnd, brcv, out_s, outb,
    silu_s, bend_s, skx_s, mt, phi, plo, y_s, gn_s, ga_s, g_s, acc, acc2, invb, mub,
    ds_s, dxw, rows, accr, accc, accv,
    ea_rcv, ea_p, la_rcv, la_p, s1, r1, own1, s2, r2, fwd2,
    in_sem, og_ss, og_rs, fa_ss, fa_rs, fb_ss, fb_rs, ba_ss, ba_rs, bb_ss, bb_rs,
    p_ss, p_rs, r1_ss, r1_rs, r2_ss, r2_rs, ea_ss, ea_rs, la_ss, la_rs,
):
    me = lax.axis_index("context")
    myt = lax.axis_index("tensor")
    mydp = lax.axis_index("dp")
    mz, mx = me // 4, me % 4
    other = 1 - mydp
    right, left = (myt + 1) % 4, (myt + 3) % 4

    barrier = pltpu.get_barrier_semaphore()

    def greet(off, carry):
        pl.semaphore_signal(
            barrier, inc=1, device_id={"context": (me + off) % CTX}, device_id_type=MESH
        )
        return carry

    pl.semaphore_signal(barrier, inc=1, device_id={"tensor": right}, device_id_type=MESH)
    pl.semaphore_signal(barrier, inc=1, device_id={"tensor": left}, device_id_type=MESH)
    lax.fori_loop(1, CTX, greet, 0)
    pl.semaphore_signal(barrier, inc=1, device_id={"dp": other}, device_id_type=MESH)

    loads = [
        pltpu.make_async_copy(src, dst, in_sem.at[i])
        for i, (src, dst) in enumerate(
            (
                (step_hbm, step_ref), (rate_hbm, rate_ref), (skip_hbm, skip_ref), (k_hbm, k_ref),
                (x_hbm, x_ref), (q_hbm, q_ref), (gain_hbm, gain_ref), (og_hbm, ogf.at[myt]),
                (gate_hbm, gate_v), (w_hbm, w_v),
            )
        )
    ]
    for copy in loads:
        copy.start()
    for copy in loads[:3]:
        copy.wait()

    raw = step_ref[...]
    eye = iota((NH, NH), 0) == iota((NH, NH), 1)
    slope = jnp.sum(jnp.where(eye, jnp.exp(rate_ref[...]), 0.0), axis=1, keepdims=True)
    step = jnp.maximum(raw, 0.0) + jnp.log(1.0 + jnp.exp(-jnp.abs(raw)))
    decay = -slope * step
    upper = (iota((T, T), 0) <= iota((T, T), 1)).astype(BF)
    cum = dot3(decay, upper)
    total = cum[:, T - 1 : T]
    stp_s[...] = step
    cum_s[...] = cum
    spread = ((iota((3 * NH, C), 0) % NH) == (iota((3 * NH, C), 1) // 64)).astype(BF)

    def expand(v, to):
        pieces = jnp.concatenate(split3(v), axis=0).astype(F32)
        turned = jnp.concatenate([pieces, jnp.zeros((W - 3 * NH, T), F32)], axis=0).T
        to[...] = dot(turned[:, : 3 * NH].astype(BF), spread)

    expand(jnp.exp(total - cum) * step, wexp)
    expand(jnp.exp(cum), eexp)
    own = (iota((NH, C), 1) // 64) == iota((NH, C), 0)
    skip_col = jnp.sum(jnp.where(eye, skip_ref[...], 0.0), axis=1, keepdims=True)
    rows[3] = jnp.sum(jnp.where(own, skip_col, 0.0), axis=0, keepdims=True)

    loads[3].wait()
    for g in range(2):
        kt[g] = k_ref[:, g * W : (g + 1) * W].T
    loads[4].wait()

    def local_state(q, carry):
        hi, lo = split2(x_ref[:, lanes(q)].astype(F32) * wexp[:, lanes(q)])
        both = dot(kt[q // 4], jnp.concatenate([hi, lo], axis=1))
        state = both[:, :W] + both[:, W:]
        factor = jnp.broadcast_to(eexp[T - 1 : T, lanes(q)], (8, W))
        snd[2 * q, 0:64] = state[0:64]
        snd[2 * q + 1, 0:64] = state[64:]
        snd[2 * q, 64:72] = factor
        snd[2 * q + 1, 64:72] = factor
        return carry

    lax.fori_loop(0, NQ, local_state, 0)

    pl.semaphore_wait(barrier, CTX + 2)

    def ctx_copy(src, dst, ss, rs, peer, src_slot, dst_slot):
        return pltpu.make_async_remote_copy(
            src_ref=src.at[src_slot],
            dst_ref=dst.at[dst_slot],
            send_sem=ss.at[src_slot],
            recv_sem=rs.at[dst_slot],
            device_id={"context": peer},
            device_id_type=MESH,
        )

    def send_all(src, dst, ss, rs):
        def one(off, carry):
            peer = (me + off) % CTX
            ctx_copy(src, dst, ss, rs, peer, peer, me).start()
            return carry

        lax.fori_loop(1, CTX, one, 0)

    def recv_all(src, dst, ss, rs):
        def one(off, carry):
            peer = (me + off) % CTX
            ctx_copy(src, dst, ss, rs, peer, peer, peer).wait_recv()
            return carry

        lax.fori_loop(1, CTX, one, 0)

    def drain_all(src, dst, ss, rs):
        def one(off, carry):
            peer = (me + off) % CTX
            ctx_copy(src, dst, ss, rs, peer, peer, me).wait_send()
            return carry

        lax.fori_loop(1, CTX, one, 0)

    def ring(src, dst, sem, peer):
        return pltpu.make_async_remote_copy(
            src_ref=src,
            dst_ref=dst,
            send_sem=og_ss.at[sem],
            recv_sem=og_rs.at[sem],
            device_id={"tensor": peer},
            device_id_type=MESH,
        )

    top, low = pl.ds(0, 128), pl.ds(128, 128)
    to_right = [ring(og_hbm.at[h], ogf.at[myt, h], i, right) for i, h in enumerate((top, low))]
    to_left = [ring(og_hbm.at[h], ogf.at[myt, h], 2 + i, left) for i, h in enumerate((low, top))]
    to_right[0].start()
    to_left[0].start()
    send_all(snd, rcv, fa_ss, fa_rs)

    to_right[1].start()
    to_left[1].start()

    expand(cum_s[...], cumx)
    loads[5].wait()
    for g in range(2):
        qg = q_ref[:, g * W : (g + 1) * W]
        qt[g] = qg.T
        sc[g] = dot_t(qg, k_ref[:, g * W : (g + 1) * W])
    causal = iota((T, T), 0) >= iota((T, T), 1)
    first = iota((T, W), 1) < 64

    def within(q, carry):
        xp = x_ref[:, lanes(q)]
        spread_tile = cumx[:, lanes(q)]
        outs = []
        for hh in range(2):
            h = 2 * q + hh
            column = spread_tile[:, 64 * hh : 64 * hh + 1]
            gap = column - cum_s[pl.ds(h, 1), :]
            m = jnp.exp(jnp.where(causal, gap, -1e30)) * stp_s[pl.ds(h, 1), :]
            mt[h] = m
            hi, lo = split2(m * sc[q // 4])
            phi[h] = hi
            plo[h] = lo
            outs.append(dot(hi, xp) + dot(lo, xp))
        y_s[:, lanes(q)] = jnp.where(first, outs[0], outs[1])
        return carry

    lax.fori_loop(0, NQ, within, 0)

    to_right[0].wait_recv()
    relay_right = ring(ogf.at[left, top], ogf.at[left, top], 4, right)
    relay_right.start()
    to_left[0].wait_recv()
    relay_left = ring(ogf.at[right, low], ogf.at[right, low], 5, left)
    relay_left.start()
    loads[8].wait()

    def gates(q, carry):
        gate = gate_v[:, lanes(q)].astype(F32)
        sig = 1.0 / (1.0 + jnp.exp(-gate))
        silu = gate * sig
        silu_s[:, lanes(q)] = silu
        bend_s[:, lanes(q)] = sig * (1.0 + gate - silu)
        skx_s[:, lanes(q)] = rows[3, :, lanes(q)] * x_ref[:, lanes(q)].astype(F32)
        return carry

    lax.fori_loop(0, NQ, gates, 0)

    rcv[me] = snd[me]
    recv_all(snd, rcv, fa_ss, fa_rs)
    run = jnp.zeros((64, W), F32)
    for s in range(CTX):
        ent_s[s] = run
        run = rcv[s, 64:65] * run + rcv[s, 0:64]
    send_all(ent_s, ent, fb_ss, fb_rs)
    ent[me] = ent_s[me]

    loads[7].wait()
    loads[9].wait()

    def pair(src, dst, sem):
        return pltpu.make_async_remote_copy(
            src_ref=src,
            dst_ref=dst,
            send_sem=p_ss.at[sem],
            recv_sem=p_rs.at[sem],
            device_id={"dp": other},
            device_id_type=MESH,
        )

    def pair_og(chunk):
        return pair(ogf.at[chunk], ogp.at[chunk % 2], chunk % 2)

    def hand_over(chunk):
        @pl.when(chunk // 2 == other)
        def _():
            pair_og(chunk).start()

        @pl.when(chunk // 2 == mydp)
        def _():
            def turn(i, carry):
                at = pl.ds(pl.multiple_of((chunk % 2) * C + i * W, W), W)
                ogt[at, 0:T] = ogf[chunk, :, lanes(i)].T
                return carry

            lax.fori_loop(0, 8, turn, 0)

    def project(chunk, first_term):
        def one(n, carry):
            where = pl.ds(pl.multiple_of(n * 256, 256), 256)
            part = dot(ogf[chunk], w_v[pl.ds(pl.multiple_of(chunk * C, C), C), where])
            gn_s[:, where] = part if first_term else gn_s[:, where] + part
            return carry

        lax.fori_loop(0, 4, one, 0)

    def take(chunk, first_term):
        hand_over(chunk)
        project(chunk, first_term)

    def turn_pair(chunk):
        @pl.when(chunk // 2 == mydp)
        def _():
            pair_og(chunk).wait_recv()

            def turn(i, carry):
                at = pl.ds(pl.multiple_of((chunk % 2) * C + i * W, W), W)
                ogt[at, T : 2 * T] = ogp[chunk % 2, :, lanes(i)].T
                return carry

            lax.fori_loop(0, 8, turn, 0)

    take(myt, True)
    loads[6].wait()
    to_right[1].wait_recv()
    take(left, False)
    turn_pair(myt)
    to_left[1].wait_recv()
    take(right, False)
    turn_pair(left)
    recv_all(ent_s, ent, fb_ss, fb_rs)

    acc[...] = jnp.zeros_like(acc)

    def entering(q):
        return jnp.concatenate([ent[2 * q], ent[2 * q + 1]], axis=0)

    def group_q(q):
        return q_ref[:, lanes(q // 4)]

    def scan_out(q, carry):
        g = q // 4
        twice = jnp.concatenate([group_q(q), group_q(q)], axis=1)
        carried = dot(twice, jnp.concatenate(split2(entering(q)), axis=0))
        y = y_s[:, lanes(q)] + eexp[:, lanes(q)] * carried
        y_s[:, lanes(q)] = y
        gated = (y + skx_s[:, lanes(q)]) * silu_s[:, lanes(q)]
        ga_s[:, lanes(q)] = gated
        acc[g] += gated * gated
        return carry

    lax.fori_loop(0, NQ, scan_out, 0)
    for g in range(2):
        mean = jnp.sum(acc[g], axis=1, keepdims=True) * (1.0 / 512)
        invb[g] = jnp.broadcast_to(lax.rsqrt(mean + EPSILON), (T, W))

    def normalize(q, carry):
        value = ga_s[:, lanes(q)] * invb[q // 4] * gain_ref[:, lanes(q)]
        nm2[0:T, lanes(q)] = value.astype(BF)
        return carry

    lax.fori_loop(0, NQ, normalize, 0)
    pair_nm = pair(nm2.at[0:T], nm2.at[T : 2 * T], 2)
    pair_nm.start()

    relay_right.wait_recv()
    relay_left.wait_recv()
    hand_over((myt + 2) % 4)
    turn_pair(right)
    turn_pair((myt + 2) % 4)
    pair_nm.wait_recv()

    def ahead(v):
        return (v + 1 + 2 * mydp) % 4

    def behind(v):
        return (v + 3 - 2 * mydp) % 4

    def far(v):
        return (v + 2) % 4

    def along(phase, half, v):
        return mz * 4 + v if phase == half else v * 4 + mx

    def mine(phase, half):
        return mx if phase == half else mz

    def place(half, j):
        v = mine(1, half)
        return (far(v), ahead(v), behind(v), v)[j]

    def weight(half, v, to, slot):
        def block(j):
            i = place(half, j)
            return (i * 4 + v) if half == 0 else (v * 4 + i)

        left_side = jnp.concatenate(
            [ogt[pl.ds(pl.multiple_of(block(i) * W, W), W), :] for i in range(4)], axis=0
        )

        def one(n, carry):
            at = pl.ds(pl.multiple_of(half * 512 + n * 256, 256), 256)
            value = dot(left_side, nm2[:, at])
            for i in range(4):
                to[slot, i, :, pl.ds(pl.multiple_of(n * 256, 256), 256)] = value[
                    i * W : (i + 1) * W
                ].astype(to.dtype)
            return carry

        lax.fori_loop(0, 2, one, 0)

    def phase1(slot, peer, part):
        at = pl.ds(2 * part, 2)
        return pltpu.make_async_remote_copy(
            src_ref=s1.at[slot, at],
            dst_ref=r1.at[slot, at],
            send_sem=r1_ss.at[2 * slot + part],
            recv_sem=r1_rs.at[2 * slot + part],
            device_id={"context": peer},
            device_id_type=MESH,
        )

    def phase2(slot, peer):
        return pltpu.make_async_remote_copy(
            src_ref=s2.at[slot],
            dst_ref=r2.at[slot],
            send_sem=r2_ss.at[slot],
            recv_sem=r2_rs.at[slot],
            device_id={"context": peer},
            device_id_type=MESH,
        )

    sends1, sends2 = [], []

    def start1(slot, peer, part):
        copy = phase1(slot, peer, part)
        copy.start()
        sends1.append(copy)

    def start2(slot, peer):
        copy = phase2(slot, peer)
        copy.start()
        sends2.append(copy)

    for half in range(2):
        v = mine(0, half)
        weight(half, far(v), s1, half)
        for part in range(2):
            start1(half, along(0, half, ahead(v)), part)

    project((myt + 2) % 4, False)
    acc2[...] = jnp.zeros_like(acc2)

    def norm_sums(q, carry):
        acc2[q // 4] += gn_s[:, lanes(q)] * gain_ref[:, lanes(q)] * ga_s[:, lanes(q)]
        return carry

    lax.fori_loop(0, NQ, norm_sums, 0)
    for g in range(2):
        inverse = invb[g]
        shift = jnp.sum(acc2[g], axis=1, keepdims=True) * (1.0 / 512)
        mub[g] = shift * inverse * inverse

    def norm_back(q, carry):
        g = q // 4
        gated = ga_s[:, lanes(q)]
        inverse = invb[g]
        gn = gn_s[:, lanes(q)]
        d_gated = inverse * (gn * gain_ref[:, lanes(q)] - gated * mub[g])
        rows[0, :, lanes(q)] = jnp.sum(gn * gated * inverse, axis=0, keepdims=True)
        xv = x_ref[:, lanes(q)].astype(F32)
        ssd = y_s[:, lanes(q)] + skx_s[:, lanes(q)]
        gg_v[:, lanes(q)] = (d_gated * ssd * bend_s[:, lanes(q)]).astype(BF)
        grad = d_gated * silu_s[:, lanes(q)]
        g_s[:, lanes(q)] = grad
        rows[1, :, lanes(q)] = jnp.sum(grad * xv, axis=0, keepdims=True)
        hi, lo = split2(eexp[:, lanes(q)] * grad)
        both = dot(qt[g], jnp.concatenate([hi, lo], axis=1))
        into = (both[:, :W] + both[:, W:]).astype(BF)
        bsnd[2 * q] = into[0:64]
        bsnd[2 * q + 1] = into[64:]
        return carry

    lax.fori_loop(0, NQ, norm_back, 0)
    send_all(bsnd, brcv, ba_ss, ba_rs)

    for half in range(2):
        weight(half, behind(mine(0, half)), s1, 2 + half)

    def send_behind(part):
        for half in range(2):
            start1(2 + half, along(0, half, behind(mine(0, half))), part)

    def relay1(part):
        for half in range(2):
            phase1(half, me, part).wait_recv()
            for i in (2 * part, 2 * part + 1):
                s1[4 + half, i] = (own1[2 + half, i] + r1[half, i].astype(F32)).astype(BF)
            start1(4 + half, along(0, half, ahead(mine(0, half))), part)

    for half in range(2):
        weight(half, ahead(mine(0, half)), own1, 2 + half)
    for half in range(2):
        weight(half, mine(0, half), own1, half)
    send_behind(0)
    relay1(0)
    brcv[me] = bsnd[me]
    recv_all(bsnd, brcv, ba_ss, ba_rs)
    run = jnp.zeros((64, W), F32)
    for s in range(CTX - 1, -1, -1):
        out_s[s] = run.astype(BF)
        run = brcv[s].astype(F32) + rcv[s, 64:65] * run
    send_all(out_s, outb, bb_ss, bb_rs)
    outb[me] = out_s[me]

    ds_s[...] = jnp.zeros_like(ds_s)
    dq_s[...] = jnp.zeros_like(dq_s)
    accr[...] = jnp.zeros_like(accr)
    accc[...] = jnp.zeros_like(accc)
    accv[...] = jnp.zeros_like(accv)

    def head_sums(q, value):
        row, lane = iota((NH, 2 * W), 0), iota((NH, 2 * W), 1) % W
        pick = (row == 2 * q + lane // 64).astype(BF)
        return dot_t(pick, jnp.concatenate(split2(value), axis=1))

    def within_back(q, carry):
        g = q // 4
        xp = x_ref[:, lanes(q)]
        grad = g_s[:, lanes(q)]
        ghi, glo = split2(grad)
        gthi, gtlo = ghi.T, glo.T
        x2 = jnp.concatenate([xp, xp], axis=1)
        zero = jnp.zeros((T, W), BF)
        parts = []
        total_ds = ds_s[g]
        for hh in range(2):
            h = 2 * q + hh
            keep = first if hh == 0 else jnp.logical_not(first)
            g2 = jnp.concatenate([jnp.where(keep, ghi, zero), jnp.where(keep, glo, zero)], axis=1)
            total_ds = total_ds + dot_t(g2, x2) * mt[h]
            a, b = gthi[64 * hh : 64 * hh + 64], gtlo[64 * hh : 64 * hh + 64]
            both = dot(jnp.concatenate([a, b], axis=0), phi[h])
            parts.append(both[0:64] + both[64:] + dot(a, plo[h]))
        ds_s[g] = total_ds
        dxw[:, lanes(q)] = jnp.concatenate(parts, axis=0).T
        accr[...] += head_sums(q, grad * y_s[:, lanes(q)])
        ehi, elo = split2(eexp[:, lanes(q)] * grad)
        shi, slo = split2(entering(q))
        to_q = dot_t(jnp.concatenate([ehi, elo], axis=1), jnp.concatenate([shi, shi], axis=1))
        dq_s[:, lanes(g)] += to_q + dot_t(ehi, slo)
        return carry

    lax.fori_loop(0, NQ, within_back, 0)
    send_behind(1)
    relay1(1)
    for g in range(2):
        hi, lo = split2(ds_s[g])
        kg = k_ref[:, g * W : (g + 1) * W]
        qg = q_ref[:, g * W : (g + 1) * W]
        dq_s[:, g * W : (g + 1) * W] += dot(hi, kg) + dot(lo, kg)
        dk_s[:, g * W : (g + 1) * W] = tdot(hi, qg) + tdot(lo, qg)

    def row_copy(src, dst, ss, rs, peer, slot):
        return pltpu.make_async_remote_copy(
            src_ref=src,
            dst_ref=dst.at[slot],
            send_sem=ss.at[peer],
            recv_sem=rs.at[slot],
            device_id={"context": peer},
            device_id_type=MESH,
        )

    def row_send(src, dst, ss, rs):
        def one(off, carry):
            row_copy(src, dst, ss, rs, (me + off) % CTX, me).start()
            return carry

        lax.fori_loop(1, CTX, one, 0)
        dst[me] = src[...]

    def row_sum(src, dst, ss, rs):
        def one(off, carry):
            row_copy(src, dst, ss, rs, (me + off) % CTX, (me + off) % CTX).wait_recv()
            return carry

        lax.fori_loop(1, CTX, one, 0)
        value = dst[0]
        for s in range(1, CTX):
            value = value + dst[s]
        return value

    def row_drain(src, dst, ss, rs):
        def one(off, carry):
            row_copy(src, dst, ss, rs, (me + off) % CTX, me).wait_send()
            return carry

        lax.fori_loop(1, CTX, one, 0)

    def as_row(column):
        at = iota((NH, W), 0) == iota((NH, W), 1)
        return jnp.sum(jnp.where(at, column, 0.0), axis=0, keepdims=True)

    ea_own[:, 0:C] = rows[0]
    ea_own[:, C : C + W] = as_row(per_head(rows[1]))
    row_send(ea_own, ea_rcv, ea_ss, ea_rs)

    recv_all(out_s, outb, bb_ss, bb_rs)

    def state_back(q, carry):
        g = q // 4
        d_state = jnp.concatenate([outb[2 * q], outb[2 * q + 1]], axis=0)
        rows[2, :, lanes(q)] = jnp.sum(
            d_state.astype(F32) * entering(q), axis=0, keepdims=True
        )
        weights = wexp[:, lanes(q)]
        xv = x_ref[:, lanes(q)].astype(F32)
        via = weights * dot(k_ref[:, lanes(g)], d_state)
        dx = dxw[:, lanes(q)] + via
        gi_v[:, lanes(q)] = (dx + rows[3, :, lanes(q)] * g_s[:, lanes(q)]).astype(BF)
        accc[...] += head_sums(q, xv * dx)
        accv[...] += head_sums(q, xv * via)
        whi, wlo = split2(weights * xv)
        twice = jnp.concatenate([d_state, d_state], axis=1)
        dk_s[:, lanes(g)] += dot_t(jnp.concatenate([whi, wlo], axis=1), twice)
        return carry

    lax.fori_loop(0, NQ, state_back, 0)

    raw = step_ref[...]
    slope = jnp.sum(jnp.where(eye, jnp.exp(rate_ref[...]), 0.0), axis=1, keepdims=True)
    step = stp_s[...]
    lower = (iota((T, T), 0) >= iota((T, T), 1)).astype(BF)
    after = dot3(accr[...] - accc[...], lower)
    log_grad = per_head(rows[2] * eexp[T - 1 : T, :])
    d_total = jnp.sum(accv[...], axis=1, keepdims=True) + log_grad
    d_decay = after + d_total
    gs_v[...] = (accc[...] / step - slope * d_decay) / (1.0 + jnp.exp(-raw))
    la_own[...] = as_row(jnp.sum(d_decay * (-slope * step), axis=1, keepdims=True))
    row_send(la_own, la_rcv, la_ss, la_rs)

    def await1(part):
        for slot in range(2, 6):
            phase1(slot, me, part).wait_recv()

    def summed(half, j):
        return own1[half, j] + r1[2 + half, j].astype(F32) + r1[4 + half, j].astype(F32)

    await1(0)
    for half in range(2):
        s2[half] = summed(half, 0).astype(BF)
        start2(half, along(1, half, ahead(mine(1, half))))
    for half in range(2):
        fwd2[half] = summed(half, 1)

    await1(1)
    for half in range(2):
        s2[2 + half] = summed(half, 2).astype(BF)
        start2(2 + half, along(1, half, behind(mine(1, half))))
    for half in range(2):
        gw_v[:, half * 512 : half * 512 + 512] = summed(half, 3)

    for half in range(2):
        phase2(half, me).wait_recv()
        s2[4 + half] = (fwd2[half] + r2[half].astype(F32)).astype(BF)
        start2(4 + half, along(1, half, ahead(mine(1, half))))
    ea_own2 = row_sum(ea_own, ea_rcv, ea_ss, ea_rs)
    row_drain(ea_own, ea_rcv, ea_ss, ea_rs)
    ea_own[...] = ea_own2
    pair_ea = pair(ea_own, ea_p, 3)
    pair_ea.start()
    drain_all(snd, rcv, fa_ss, fa_rs)
    drain_all(ent_s, ent, fb_ss, fb_rs)
    drain_all(bsnd, brcv, ba_ss, ba_rs)
    drain_all(out_s, outb, bb_ss, bb_rs)

    la_own2 = row_sum(la_own, la_rcv, la_ss, la_rs)
    row_drain(la_own, la_rcv, la_ss, la_rs)
    la_own[...] = la_own2
    pair_la = pair(la_own, la_p, 4)
    pair_la.start()
    pair_ea.wait()
    ea_own[...] += ea_p[...]
    pair_la.wait()
    la_own[...] += la_p[...]
    for copy in (*to_right, *to_left, relay_right, relay_left, pair_nm, *sends1):
        copy.wait_send()
    for i in range(2):
        pair_og(2 * other + i).wait_send()
    for half in range(2):
        at = slice(half * 512, half * 512 + 512)
        phase2(2 + half, me).wait_recv()
        gw_v[:, at] += r2[2 + half].astype(F32)
    for half in range(2):
        at = slice(half * 512, half * 512 + 512)
        phase2(4 + half, me).wait_recv()
        gw_v[:, at] += r2[4 + half].astype(F32)
    for copy in sends2:
        copy.wait_send()


def hand_out(
    gi_v, gg_v, gk_v, gq_v, gs_v, gw_v, early_v, late_v,
    gi_out, gg_out, gk_out, gq_out, gs_out, gw_out, rate_ref, skip_ref, norm_ref, out_sem,
):
    ways = (
        (gi_v, gi_out), (gg_v, gg_out), (gw_v, gw_out), (gk_v, gk_out), (gq_v, gq_out),
        (gs_v, gs_out),
    )
    out = [pltpu.make_async_copy(*way, out_sem.at[i]) for i, way in enumerate(ways)]
    for copy in out:
        copy.start()
    norm_ref[...] = early_v[:, 0:C]
    skip_ref[...] = early_v[:, C : C + NH]
    rate_ref[...] = late_v[:, 0:NH]
    for copy in out:
        copy.wait()


def body(
    ssm_input, gate_input, state_keys, state_queries, step_raw,
    rate_log, skip_gain, norm_gain, out_weight, out_grad,
):
    vmem, anywhere = pl.BlockSpec(memory_space=pltpu.VMEM), pl.BlockSpec(memory_space=pl.ANY)
    V, S = pltpu.VMEM, pltpu.SemaphoreType.DMA
    shape = jax.ShapeDtypeStruct
    wide, by_pos, per_ctx = V((T, C), F32), V((2, T, W), F32), V((CTX, 64, W), BF)
    scratch = [
        V((T, C), BF), V((T, 2 * W), BF), V((T, 2 * W), BF), V((NH, T), F32), V((1, NH), F32),
        V((1, NH), F32), V((1, C), F32),
        V((T, C), BF), V((4 * C, C), BF), V((4, T, C), BF), V((2, T, C), BF), V((2 * C, 2 * T), BF),
        V((2 * T, C), BF),
        wide, wide, wide, V((NH, T), F32), V((NH, T), F32), V((2, W, T), BF), V((2, W, T), BF),
        V((2, T, T), F32),
        V((CTX, 72, W), F32), V((CTX, 72, W), F32), V((CTX, 64, W), F32), V((CTX, 64, W), F32),
        per_ctx, per_ctx, per_ctx, per_ctx,
        wide, wide, wide, V((NH, T, T), F32), V((NH, T, T), BF), V((NH, T, T), BF),
        wide, wide, wide, wide, by_pos, by_pos, by_pos, by_pos,
        V((2, T, T), F32), wide,
        V((4, 1, C), F32), V((NH, T), F32), V((NH, T), F32), V((NH, T), F32),
        V((CTX, 1, C + W), F32), V((1, C + W), F32), V((CTX, 1, W), F32), V((1, W), F32),
        V((6, 4, W, 512), BF), V((6, 4, W, 512), BF), V((4, 4, W, 512), F32),
        V((6, W, 512), BF), V((6, W, 512), BF), V((2, W, 512), F32),
        S((10,)), S((6,)), S((6,)), *[S((CTX,))] * 8,
        S((5,)), S((5,)), S((12,)), S((12,)), S((6,)), S((6,)), *[S((CTX,))] * 4,
    ]
    parts = pl.pallas_call(
        kernel,
        out_shape=(
            V((T, C), BF), V((T, C), BF), V((T, 2 * W), F32), V((T, 2 * W), F32),
            V((NH, T), F32), V((W, C), F32), V((1, C + W), F32), V((1, W), F32),
        ),
        in_specs=[anywhere] * 10,
        out_specs=[vmem] * 8,
        scratch_shapes=scratch,
        compiler_params=pltpu.CompilerParams(
            collective_id=0, has_side_effects=True, vmem_limit_bytes=60 * 1024 * 1024
        ),
    )(
        ssm_input[0], state_keys[0], state_queries[0], step_raw[0],
        rate_log.reshape(1, NH), skip_gain.reshape(1, NH), norm_gain.reshape(1, C),
        gate_input[0], out_weight, out_grad[0],
    )
    gi, gg, gk, gq, gs, gw, rate, skip, norm = pl.pallas_call(
        hand_out,
        out_shape=(
            shape((T, C), BF), shape((T, C), BF), shape((T, 2 * W), F32), shape((T, 2 * W), F32),
            shape((NH, T), F32), shape((W, C), F32),
            shape((1, NH), F32), shape((1, NH), F32), shape((1, C), F32),
        ),
        in_specs=[vmem] * 8,
        out_specs=[anywhere] * 6 + [vmem] * 3,
        scratch_shapes=[S((6,))],
    )(*[pltpu.with_memory_space_constraint(p, pltpu.VMEM) for p in parts])
    return (
        gi[None], gg[None], gk[None], gq[None], gs[None],
        rate.reshape(NH), skip.reshape(NH), norm.reshape(C), gw,
    )


def solution(mesh):
    return jax.shard_map(
        body,
        mesh=mesh,
        in_specs=(
            P("dp", "context", "tensor"),
            P("dp", "context", "tensor"),
            P("dp", "context", "tensor"),
            P("dp", "context", "tensor"),
            P("dp", "tensor", "context"),
            P("tensor"),
            P("tensor"),
            P("tensor"),
            P(None, "tensor"),
            P("dp", "context", "tensor"),
        ),
        out_specs=(
            P("dp", "context", "tensor"),
            P("dp", "context", "tensor"),
            P("dp", "context", "tensor"),
            P("dp", "context", "tensor"),
            P("dp", "tensor", "context"),
            P("tensor"),
            P("tensor"),
            P("tensor"),
            P(("dp", "context"), "tensor"),
        ),
        check_vma=False,
    )
```

time: 106 us -> 70.9 us (0.67)
  Pallas kernels: 91.5 us -> 70.1 us
  local copies, waits for them, and re-layouts: 13 us -> 0 us
    pallas_call x1 -> x2, Pallas kernels: 91.5 us -> 70.1 us  [the longest x1 68.1 us: body(): pl.pallas_call(kernel, out_shape=(V((T, C), BF), V((T, C), BF), V((T, 2 *...]
    unnamed x6 -> x0, local copies, waits for them, and re-layouts: 10.3 us -> none
    slice x1 -> x0, local copies, waits for them, and re-layouts: 1.47 us -> none  [body(): sm[0:NH, 1]]
    reshape x1 -> x0, local copies, waits for them, and re-layouts: 1.27 us -> none  [body(): sm[NH:24].reshape(C)]
where the time goes in v2:
time: 70.9 us; the launch traced here: 70.7 us
  Pallas kernels  70.1 us (99%)
    pallas_call x1, Pallas kernels, body(): pl.pallas_call(kernel, out_shape=(V((T, C), BF), V((T, C), BF), V((T, 2 *...  68.1 us
    pallas_call x1, Pallas kernels, body(): pl.pallas_call(hand_out, out_shape=(shape((T, C), BF), shape((T, C), BF),...  1.97 us

profile of v2, /device:TPU:1, one launch (start us, length us, event | category | flops | bytes accessed | tf_op | source)
XLA Modules:
  0.0 70.7 jit_solution(8423772051371436592)
XLA Ops:
  0.6 68.1 %shard_map.169 = (bf16[256,1024]{1,0:T(8,128)(2,1)S(1)}, bf16[256,1024]{1,0:T(8,128)(2,1)S(1)}, f32[256,256]{1,0:T(8,128)S(1)}, f32[256,256]{1,0:T(8,128)S(1)}, ...) custom-call(bf16[256,1024]{1,0:T(8,128)(2,1)} %bitcast.17, ...), custom_call_target="tpu_custom_call" | custom-call | tf_op jit(solution)/shard_map/pallas_call | solution.py:743
  68.8 2.0 %shard_map.170 = (bf16[256,1024]{1,0:T(8,128)(2,1)}, bf16[256,1024]{1,0:T(8,128)(2,1)}, f32[256,256]{1,0:T(8,128)}, f32[256,256]{1,0:T(8,128)}, f32[16,256]{1,0:...) custom-call(bf16[256,1024]{1,0:T(8,128)(2,1)S(1)} %get-tuple-element.26.gi_v, ...), custom_call_target="tpu_custom_call" | custom-call | tf_op jit(solution)/shard_map/pallas_call | solution.py:760

commit v3 on v2

--- a/solution.py
+++ b/solution.py
@@ -69,9 +69,8 @@
     snd, rcv, ent_s, ent, bsnd, brcv, out_s, outb,
     silu_s, bend_s, skx_s, mt, phi, plo, y_s, gn_s, ga_s, g_s, acc, acc2, invb, mub,
     ds_s, dxw, rows, accr, accc, accv,
-    ea_rcv, ea_p, la_rcv, la_p, s1, r1, own1, s2, r2, fwd2,
-    in_sem, og_ss, og_rs, fa_ss, fa_rs, fb_ss, fb_rs, ba_ss, ba_rs, bb_ss, bb_rs,
-    p_ss, p_rs, r1_ss, r1_rs, r2_ss, r2_rs, ea_ss, ea_rs, la_ss, la_rs,
+    ea_rcv, ea_p, la_rcv, la_p, s1, r1, own1, s2, r2,
+    in_sem, og_ss, og_rs, leg_ss, leg_rs, p_ss, p_rs, r1_ss, r1_rs, r2_ss, r2_rs,
 ):
     me = lax.axis_index("context")
     myt = lax.axis_index("tensor")
@@ -151,45 +150,37 @@
 
     pl.semaphore_wait(barrier, CTX + 2)
 
-    def ctx_copy(src, dst, ss, rs, peer, src_slot, dst_slot):
-        return pltpu.make_async_remote_copy(
-            src_ref=src.at[src_slot],
-            dst_ref=dst.at[dst_slot],
-            send_sem=ss.at[src_slot],
-            recv_sem=rs.at[dst_slot],
-            device_id={"context": peer},
-            device_id_type=MESH,
-        )
-
-    def send_all(src, dst, ss, rs):
+    def send_all(src, dst, leg):
         def one(off, carry):
             peer = (me + off) % CTX
-            ctx_copy(src, dst, ss, rs, peer, peer, me).start()
+            pltpu.make_async_remote_copy(
+                src_ref=src.at[peer],
+                dst_ref=dst.at[me],
+                send_sem=leg_ss.at[leg],
+                recv_sem=leg_rs.at[leg],
+                device_id={"context": peer},
+                device_id_type=MESH,
+            ).start()
             return carry
 
         lax.fori_loop(1, CTX, one, 0)
 
-    def recv_all(src, dst, ss, rs):
-        def one(off, carry):
-            peer = (me + off) % CTX
-            ctx_copy(src, dst, ss, rs, peer, peer, peer).wait_recv()
-            return carry
-
-        lax.fori_loop(1, CTX, one, 0)
-
-    def drain_all(src, dst, ss, rs):
-        def one(off, carry):
-            peer = (me + off) % CTX
-            ctx_copy(src, dst, ss, rs, peer, peer, me).wait_send()
-            return carry
-
-        lax.fori_loop(1, CTX, one, 0)
+    def all_of(slots, leg):
+        some = slots.at[pl.ds(0, CTX - 1)]
+        return pltpu.make_async_remote_copy(
+            src_ref=some,
+            dst_ref=some,
+            send_sem=leg_ss.at[leg],
+            recv_sem=leg_rs.at[leg],
+            device_id={"context": (me + 1) % CTX},
+            device_id_type=MESH,
+        )
 
     def ring(src, dst, sem, peer):
         return pltpu.make_async_remote_copy(
             src_ref=src,
             dst_ref=dst,
-            send_sem=og_ss.at[sem],
+            send_sem=og_ss.at[0],
             recv_sem=og_rs.at[sem],
             device_id={"tensor": peer},
             device_id_type=MESH,
@@ -200,7 +191,7 @@
     to_left = [ring(og_hbm.at[h], ogf.at[myt, h], 2 + i, left) for i, h in enumerate((low, top))]
     to_right[0].start()
     to_left[0].start()
-    send_all(snd, rcv, fa_ss, fa_rs)
+    send_all(snd, rcv, 0)
 
     to_right[1].start()
     to_left[1].start()
@@ -233,11 +224,20 @@
 
     lax.fori_loop(0, NQ, within, 0)
 
+    rcv[me] = snd[me]
+    all_of(rcv, 0).wait_recv()
+    run = jnp.zeros((64, W), F32)
+    for s in range(CTX):
+        ent_s[s] = run
+        run = rcv[s, 64:65] * run + rcv[s, 0:64]
+    send_all(ent_s, ent, 1)
+    ent[me] = ent_s[me]
+
     to_right[0].wait_recv()
     relay_right = ring(ogf.at[left, top], ogf.at[left, top], 4, right)
     relay_right.start()
     to_left[0].wait_recv()
-    relay_left = ring(ogf.at[right, low], ogf.at[right, low], 5, left)
+    relay_left = ring(ogf.at[right, low], ogf.at[right, low], 4, left)
     relay_left.start()
     loads[8].wait()
 
@@ -251,15 +251,6 @@
         return carry
 
     lax.fori_loop(0, NQ, gates, 0)
-
-    rcv[me] = snd[me]
-    recv_all(snd, rcv, fa_ss, fa_rs)
-    run = jnp.zeros((64, W), F32)
-    for s in range(CTX):
-        ent_s[s] = run
-        run = rcv[s, 64:65] * run + rcv[s, 0:64]
-    send_all(ent_s, ent, fb_ss, fb_rs)
-    ent[me] = ent_s[me]
 
     loads[7].wait()
     loads[9].wait()
@@ -319,12 +310,14 @@
     take(myt, True)
     loads[6].wait()
     to_right[1].wait_recv()
-    take(left, False)
+    to_left[1].wait_recv()
+    hand_over(left)
+    hand_over(right)
     turn_pair(myt)
-    to_left[1].wait_recv()
-    take(right, False)
+    project(left, False)
     turn_pair(left)
-    recv_all(ent_s, ent, fb_ss, fb_rs)
+    turn_pair(right)
+    all_of(ent, 1).wait_recv()
 
     acc[...] = jnp.zeros_like(acc)
 
@@ -359,10 +352,9 @@
     pair_nm = pair(nm2.at[0:T], nm2.at[T : 2 * T], 2)
     pair_nm.start()
 
-    relay_right.wait_recv()
-    relay_left.wait_recv()
+    ring(ogf.at[0], ogf.at[0], 4, right).wait_recv()
     hand_over((myt + 2) % 4)
-    turn_pair(right)
+    project(right, False)
     turn_pair((myt + 2) % 4)
     pair_nm.wait_recv()
 
@@ -410,8 +402,8 @@
         return pltpu.make_async_remote_copy(
             src_ref=s1.at[slot, at],
             dst_ref=r1.at[slot, at],
-            send_sem=r1_ss.at[2 * slot + part],
-            recv_sem=r1_rs.at[2 * slot + part],
+            send_sem=r1_ss.at[0],
+            recv_sem=r1_rs.at[part if slot > 1 else 2 + 2 * slot + part],
             device_id={"context": peer},
             device_id_type=MESH,
         )
@@ -420,23 +412,36 @@
         return pltpu.make_async_remote_copy(
             src_ref=s2.at[slot],
             dst_ref=r2.at[slot],
-            send_sem=r2_ss.at[slot],
-            recv_sem=r2_rs.at[slot],
+            send_sem=r2_ss.at[0],
+            recv_sem=r2_rs.at[0],
             device_id={"context": peer},
             device_id_type=MESH,
         )
 
-    sends1, sends2 = [], []
-
     def start1(slot, peer, part):
-        copy = phase1(slot, peer, part)
-        copy.start()
-        sends1.append(copy)
+        phase1(slot, peer, part).start()
 
     def start2(slot, peer):
-        copy = phase2(slot, peer)
-        copy.start()
-        sends2.append(copy)
+        phase2(slot, peer).start()
+
+    def every1(ref, sem):
+        return pltpu.make_async_remote_copy(
+            src_ref=s1,
+            dst_ref=ref,
+            send_sem=r1_ss.at[0],
+            recv_sem=r1_rs.at[sem],
+            device_id={"context": (me + 1) % CTX},
+            device_id_type=MESH,
+        )
+
+    every2 = pltpu.make_async_remote_copy(
+        src_ref=s2,
+        dst_ref=r2,
+        send_sem=r2_ss.at[0],
+        recv_sem=r2_rs.at[0],
+        device_id={"context": (me + 1) % CTX},
+        device_id_type=MESH,
+    )
 
     for half in range(2):
         v = mine(0, half)
@@ -478,7 +483,7 @@
         return carry
 
     lax.fori_loop(0, NQ, norm_back, 0)
-    send_all(bsnd, brcv, ba_ss, ba_rs)
+    send_all(bsnd, brcv, 2)
 
     for half in range(2):
         weight(half, behind(mine(0, half)), s1, 2 + half)
@@ -501,12 +506,12 @@
     send_behind(0)
     relay1(0)
     brcv[me] = bsnd[me]
-    recv_all(bsnd, brcv, ba_ss, ba_rs)
+    all_of(brcv, 2).wait_recv()
     run = jnp.zeros((64, W), F32)
     for s in range(CTX - 1, -1, -1):
         out_s[s] = run.astype(BF)
         run = brcv[s].astype(F32) + rcv[s, 64:65] * run
-    send_all(out_s, outb, bb_ss, bb_rs)
+    send_all(out_s, outb, 3)
     outb[me] = out_s[me]
 
     ds_s[...] = jnp.zeros_like(ds_s)
@@ -557,41 +562,29 @@
         dq_s[:, g * W : (g + 1) * W] += dot(hi, kg) + dot(lo, kg)
         dk_s[:, g * W : (g + 1) * W] = tdot(hi, qg) + tdot(lo, qg)
 
-    def row_copy(src, dst, ss, rs, peer, slot):
-        return pltpu.make_async_remote_copy(
-            src_ref=src,
-            dst_ref=dst.at[slot],
-            send_sem=ss.at[peer],
-            recv_sem=rs.at[slot],
-            device_id={"context": peer},
-            device_id_type=MESH,
-        )
-
-    def row_send(src, dst, ss, rs):
+    def row_send(src, dst, leg):
         def one(off, carry):
-            row_copy(src, dst, ss, rs, (me + off) % CTX, me).start()
+            peer = (me + off) % CTX
+            pltpu.make_async_remote_copy(
+                src_ref=src,
+                dst_ref=dst.at[me],
+                send_sem=leg_ss.at[leg],
+                recv_sem=leg_rs.at[leg],
+                device_id={"context": peer},
+                device_id_type=MESH,
+            ).start()
             return carry
 
         lax.fori_loop(1, CTX, one, 0)
         dst[me] = src[...]
 
-    def row_sum(src, dst, ss, rs):
-        def one(off, carry):
-            row_copy(src, dst, ss, rs, (me + off) % CTX, (me + off) % CTX).wait_recv()
-            return carry
-
-        lax.fori_loop(1, CTX, one, 0)
+    def row_sum(src, dst, leg):
+        all_of(dst, leg).wait_recv()
         value = dst[0]
-        for s in range(1, CTX):
-            value = value + dst[s]
-        return value
-
-    def row_drain(src, dst, ss, rs):
-        def one(off, carry):
-            row_copy(src, dst, ss, rs, (me + off) % CTX, me).wait_send()
-            return carry
-
-        lax.fori_loop(1, CTX, one, 0)
+        for i in range(1, CTX):
+            value = value + dst[i]
+        all_of(dst, leg).wait_send()
+        src[...] = value
 
     def as_row(column):
         at = iota((NH, W), 0) == iota((NH, W), 1)
@@ -599,9 +592,9 @@
 
     ea_own[:, 0:C] = rows[0]
     ea_own[:, C : C + W] = as_row(per_head(rows[1]))
-    row_send(ea_own, ea_rcv, ea_ss, ea_rs)
-
-    recv_all(out_s, outb, bb_ss, bb_rs)
+    row_send(ea_own, ea_rcv, 4)
+
+    all_of(outb, 3).wait_recv()
 
     def state_back(q, carry):
         g = q // 4
@@ -633,66 +626,55 @@
     d_decay = after + d_total
     gs_v[...] = (accc[...] / step - slope * d_decay) / (1.0 + jnp.exp(-raw))
     la_own[...] = as_row(jnp.sum(d_decay * (-slope * step), axis=1, keepdims=True))
-    row_send(la_own, la_rcv, la_ss, la_rs)
+    row_send(la_own, la_rcv, 5)
 
     def await1(part):
-        for slot in range(2, 6):
-            phase1(slot, me, part).wait_recv()
+        every1(r1.at[pl.ds(2, 4), pl.ds(2 * part, 2)], part).wait_recv()
 
     def summed(half, j):
         return own1[half, j] + r1[2 + half, j].astype(F32) + r1[4 + half, j].astype(F32)
 
     await1(0)
     for half in range(2):
-        s2[half] = summed(half, 0).astype(BF)
-        start2(half, along(1, half, ahead(mine(1, half))))
-    for half in range(2):
-        fwd2[half] = summed(half, 1)
+        v = mine(1, half)
+        for j, there in ((0, far(v)), (1, ahead(v))):
+            s2[2 * j + half] = summed(half, j).astype(BF)
+            start2(2 * j + half, along(1, half, there))
 
     await1(1)
     for half in range(2):
-        s2[2 + half] = summed(half, 2).astype(BF)
-        start2(2 + half, along(1, half, behind(mine(1, half))))
+        s2[4 + half] = summed(half, 2).astype(BF)
+        start2(4 + half, along(1, half, behind(mine(1, half))))
     for half in range(2):
         gw_v[:, half * 512 : half * 512 + 512] = summed(half, 3)
 
-    for half in range(2):
-        phase2(half, me).wait_recv()
-        s2[4 + half] = (fwd2[half] + r2[half].astype(F32)).astype(BF)
-        start2(4 + half, along(1, half, ahead(mine(1, half))))
-    ea_own2 = row_sum(ea_own, ea_rcv, ea_ss, ea_rs)
-    row_drain(ea_own, ea_rcv, ea_ss, ea_rs)
-    ea_own[...] = ea_own2
+    row_sum(la_own, la_rcv, 5)
+    pair_la = pair(la_own, la_p, 4)
+    pair_la.start()
+    row_sum(ea_own, ea_rcv, 4)
     pair_ea = pair(ea_own, ea_p, 3)
     pair_ea.start()
-    drain_all(snd, rcv, fa_ss, fa_rs)
-    drain_all(ent_s, ent, fb_ss, fb_rs)
-    drain_all(bsnd, brcv, ba_ss, ba_rs)
-    drain_all(out_s, outb, bb_ss, bb_rs)
-
-    la_own2 = row_sum(la_own, la_rcv, la_ss, la_rs)
-    row_drain(la_own, la_rcv, la_ss, la_rs)
-    la_own[...] = la_own2
-    pair_la = pair(la_own, la_p, 4)
-    pair_la.start()
+    all_of(rcv, 0).wait_send()
+    all_of(ent, 1).wait_send()
+    all_of(brcv, 2).wait_send()
+    all_of(outb, 3).wait_send()
+
     pair_ea.wait()
     ea_own[...] += ea_p[...]
     pair_la.wait()
     la_own[...] += la_p[...]
-    for copy in (*to_right, *to_left, relay_right, relay_left, pair_nm, *sends1):
-        copy.wait_send()
+    ring(ogf.at[pl.ds(0, 3)], ogf.at[pl.ds(0, 3)], 4, right).wait_send()
+    pair_nm.wait_send()
+    every1(r1, 0).wait_send()
     for i in range(2):
         pair_og(2 * other + i).wait_send()
+    every2.wait_recv()
     for half in range(2):
         at = slice(half * 512, half * 512 + 512)
-        phase2(2 + half, me).wait_recv()
-        gw_v[:, at] += r2[2 + half].astype(F32)
-    for half in range(2):
-        at = slice(half * 512, half * 512 + 512)
-        phase2(4 + half, me).wait_recv()
-        gw_v[:, at] += r2[4 + half].astype(F32)
-    for copy in sends2:
-        copy.wait_send()
+        gw_v[:, at] += (
+            r2[half].astype(F32) + r2[2 + half].astype(F32) + r2[4 + half].astype(F32)
+        )
+    every2.wait_send()
 
 
 def hand_out(
@@ -736,9 +718,9 @@
         V((4, 1, C), F32), V((NH, T), F32), V((NH, T), F32), V((NH, T), F32),
         V((CTX, 1, C + W), F32), V((1, C + W), F32), V((CTX, 1, W), F32), V((1, W), F32),
         V((6, 4, W, 512), BF), V((6, 4, W, 512), BF), V((4, 4, W, 512), F32),
-        V((6, W, 512), BF), V((6, W, 512), BF), V((2, W, 512), F32),
-        S((10,)), S((6,)), S((6,)), *[S((CTX,))] * 8,
-        S((5,)), S((5,)), S((12,)), S((12,)), S((6,)), S((6,)), *[S((CTX,))] * 4,
+        V((6, W, 512), BF), V((6, W, 512), BF),
+        S((10,)), S((1,)), S((5,)), S((6,)), S((6,)),
+        S((5,)), S((5,)), S((1,)), S((6,)), S((1,)), S((1,)),
     ]
     parts = pl.pallas_call(
         kernel,

time: 70.9 us -> 67.3 us (0.949)
  Pallas kernels: 70.1 us -> 66.5 us
    pallas_call x1, Pallas kernels: 68.1 us -> 64.5 us  [body(): pl.pallas_call(kernel, out_shape=(V((T, C), BF), V((T, C), BF), V((T, 2 *...]
where the time goes in v3:
time: 67.3 us; the launch traced here: 67.1 us
  Pallas kernels  66.5 us (99%)
    pallas_call x1, Pallas kernels, body(): pl.pallas_call(kernel, out_shape=(V((T, C), BF), V((T, C), BF), V((T, 2 *...  64.5 us
    pallas_call x1, Pallas kernels, body(): pl.pallas_call(hand_out, out_shape=(shape((T, C), BF), shape((T, C), BF),...  1.97 us

profile of v3, /device:TPU:1, one launch (start us, length us, event | category | flops | bytes accessed | tf_op | source)
XLA Modules:
  0.0 67.1 jit_solution(5953107299503166576)
XLA Ops:
  0.6 64.5 %shard_map.169 = (bf16[256,1024]{1,0:T(8,128)(2,1)S(1)}, bf16[256,1024]{1,0:T(8,128)(2,1)S(1)}, f32[256,256]{1,0:T(8,128)S(1)}, f32[256,256]{1,0:T(8,128)S(1)}, ...) custom-call(bf16[256,1024]{1,0:T(8,128)(2,1)} %bitcast.17, ...), custom_call_target="tpu_custom_call" | custom-call | tf_op jit(solution)/shard_map/pallas_call | solution.py:725
  65.1 2.0 %shard_map.170 = (bf16[256,1024]{1,0:T(8,128)(2,1)}, bf16[256,1024]{1,0:T(8,128)(2,1)}, f32[256,256]{1,0:T(8,128)}, f32[256,256]{1,0:T(8,128)}, f32[16,256]{1,0:...) custom-call(bf16[256,1024]{1,0:T(8,128)(2,1)S(1)} %get-tuple-element.26.gi_v, ...), custom_call_target="tpu_custom_call" | custom-call | tf_op jit(solution)/shard_map/pallas_call | solution.py:742

commit v4 on v3

--- a/solution.py
+++ b/solution.py
@@ -16,6 +16,10 @@
 NQ = 8
 W = 128
 CTX = 16
+FAR_FIRST = sorted(
+    [(dx, dz) for dx in range(4) for dz in range(4) if dx or dz],
+    key=lambda d: -min(d[0], 4 - d[0]) - min(d[1], 4 - d[1]),
+)
 
 
 def dot(a, b):
@@ -70,7 +74,7 @@
     silu_s, bend_s, skx_s, mt, phi, plo, y_s, gn_s, ga_s, g_s, acc, acc2, invb, mub,
     ds_s, dxw, rows, accr, accc, accv,
     ea_rcv, ea_p, la_rcv, la_p, s1, r1, own1, s2, r2,
-    in_sem, og_ss, og_rs, leg_ss, leg_rs, p_ss, p_rs, r1_ss, r1_rs, r2_ss, r2_rs,
+    in_sem, og_ss, og_rs, leg_ss, leg_rs, ea_ss, ea_rs, p_ss, p_rs, r1_ss, r1_rs, r2_ss, r2_rs,
 ):
     me = lax.axis_index("context")
     myt = lax.axis_index("tensor")
@@ -151,8 +155,8 @@
     pl.semaphore_wait(barrier, CTX + 2)
 
     def send_all(src, dst, leg):
-        def one(off, carry):
-            peer = (me + off) % CTX
+        for dx, dz in FAR_FIRST:
+            peer = (mz + dz) % 4 * 4 + (mx + dx) % 4
             pltpu.make_async_remote_copy(
                 src_ref=src.at[peer],
                 dst_ref=dst.at[me],
@@ -161,9 +165,6 @@
                 device_id={"context": peer},
                 device_id_type=MESH,
             ).start()
-            return carry
-
-        lax.fori_loop(1, CTX, one, 0)
 
     def all_of(slots, leg):
         some = slots.at[pl.ds(0, CTX - 1)]
@@ -586,13 +587,41 @@
         all_of(dst, leg).wait_send()
         src[...] = value
 
+    def line_send(stage):
+        spot = mz if stage else mx
+        for d in (2, 1, 3):
+            there = (spot + d) % 4
+            pltpu.make_async_remote_copy(
+                src_ref=ea_rcv.at[stage, spot],
+                dst_ref=ea_rcv.at[stage, spot],
+                send_sem=ea_ss.at[stage],
+                recv_sem=ea_rs.at[stage],
+                device_id={"context": there * 4 + mx if stage else mz * 4 + there},
+                device_id_type=MESH,
+            ).start()
+
+    def line_sum(stage):
+        some = ea_rcv.at[stage, pl.ds(0, 3)]
+        whole = pltpu.make_async_remote_copy(
+            src_ref=some,
+            dst_ref=some,
+            send_sem=ea_ss.at[stage],
+            recv_sem=ea_rs.at[stage],
+            device_id={"context": (me + 1) % CTX},
+            device_id_type=MESH,
+        )
+        whole.wait_recv()
+        whole.wait_send()
+        return ea_rcv[stage, 0] + ea_rcv[stage, 1] + ea_rcv[stage, 2] + ea_rcv[stage, 3]
+
     def as_row(column):
         at = iota((NH, W), 0) == iota((NH, W), 1)
         return jnp.sum(jnp.where(at, column, 0.0), axis=0, keepdims=True)
 
     ea_own[:, 0:C] = rows[0]
     ea_own[:, C : C + W] = as_row(per_head(rows[1]))
-    row_send(ea_own, ea_rcv, 4)
+    ea_rcv[0, mx] = ea_own[...]
+    line_send(0)
 
     all_of(outb, 3).wait_recv()
 
@@ -648,10 +677,12 @@
     for half in range(2):
         gw_v[:, half * 512 : half * 512 + 512] = summed(half, 3)
 
+    ea_rcv[1, mz] = line_sum(0)
+    line_send(1)
     row_sum(la_own, la_rcv, 5)
     pair_la = pair(la_own, la_p, 4)
     pair_la.start()
-    row_sum(ea_own, ea_rcv, 4)
+    ea_own[...] = line_sum(1)
     pair_ea = pair(ea_own, ea_p, 3)
     pair_ea.start()
     all_of(rcv, 0).wait_send()
@@ -716,10 +747,10 @@
         wide, wide, wide, wide, by_pos, by_pos, by_pos, by_pos,
         V((2, T, T), F32), wide,
         V((4, 1, C), F32), V((NH, T), F32), V((NH, T), F32), V((NH, T), F32),
-        V((CTX, 1, C + W), F32), V((1, C + W), F32), V((CTX, 1, W), F32), V((1, W), F32),
+        V((2, 4, 1, C + W), F32), V((1, C + W), F32), V((CTX, 1, W), F32), V((1, W), F32),
         V((6, 4, W, 512), BF), V((6, 4, W, 512), BF), V((4, 4, W, 512), F32),
         V((6, W, 512), BF), V((6, W, 512), BF),
-        S((10,)), S((1,)), S((5,)), S((6,)), S((6,)),
+        S((10,)), S((1,)), S((5,)), S((6,)), S((6,)), S((2,)), S((2,)),
         S((5,)), S((5,)), S((1,)), S((6,)), S((1,)), S((1,)),
     ]
     parts = pl.pallas_call(

time: 67.3 us -> 67.7 us (level)
  no operation moved by 1% of the time
where the time goes in v4:
time: 67.7 us; the launch traced here: 67.6 us
  Pallas kernels  66.9 us (99%)
    pallas_call x1, Pallas kernels, body(): pl.pallas_call(kernel, out_shape=(V((T, C), BF), V((T, C), BF), V((T, 2 *...  64.9 us
    pallas_call x1, Pallas kernels, body(): pl.pallas_call(hand_out, out_shape=(shape((T, C), BF), shape((T, C), BF),...  1.97 us

profile of v4, /device:TPU:1, one launch (start us, length us, event | category | flops | bytes accessed | tf_op | source)
XLA Modules:
  0.0 67.6 jit_solution(298057407022750111)
XLA Ops:
  0.6 64.9 %shard_map.169 = (bf16[256,1024]{1,0:T(8,128)(2,1)S(1)}, bf16[256,1024]{1,0:T(8,128)(2,1)S(1)}, f32[256,256]{1,0:T(8,128)S(1)}, f32[256,256]{1,0:T(8,128)S(1)}, ...) custom-call(bf16[256,1024]{1,0:T(8,128)(2,1)} %bitcast.17, ...), custom_call_target="tpu_custom_call" | custom-call | tf_op jit(solution)/shard_map/pallas_call | solution.py:756
  65.6 2.0 %shard_map.170 = (bf16[256,1024]{1,0:T(8,128)(2,1)}, bf16[256,1024]{1,0:T(8,128)(2,1)}, f32[256,256]{1,0:T(8,128)}, f32[256,256]{1,0:T(8,128)}, f32[16,256]{1,0:...) custom-call(bf16[256,1024]{1,0:T(8,128)(2,1)S(1)} %get-tuple-element.26.gi_v, ...), custom_call_target="tpu_custom_call" | custom-call | tf_op jit(solution)/shard_map/pallas_call | solution.py:773
